TPU v7x, 256 devices: a whole 4x4x8 slice. The times are simulated.
256 devices in a mesh: grp: 8 (over x, core), tile: 32 (over y, z).
Axes of the slice: x: 4, y: 4, z: 8, core: 2. Of those that a mesh axis runs over, the one named last changes fastest.
Arguments:
- nodes: bfloat16 [262144, 192], P(('grp', 'tile')), may hold values from -6 to 6
- node_ids: int32 [262144], P(('grp', 'tile')), may hold values from 0 to 262143
- node_count: int32 [256], P(('grp', 'tile')), may hold values from 256 to 1024
- pos_weight: float32 [3, 192], replicated, may hold values from -6 to 6
- gain_one: float32 [192], replicated, may hold values from 0.25 to 1.75
- qkv_one: bfloat16 [192, 576], replicated, may hold values from -0.4375 to 0.4375
- out_one: bfloat16 [192, 192], replicated, may hold values from -0.4375 to 0.4375
- gain_two: float32 [192], replicated, may hold values from 0.25 to 1.75
- qkv_two: bfloat16 [192, 576], replicated, may hold values from -0.4375 to 0.4375
- out_two: bfloat16 [192, 192], replicated, may hold values from -0.4375 to 0.4375
- gain_three: float32 [192], replicated, may hold values from 0.25 to 1.75
- w_up: bfloat16 [192, 768], replicated, may hold values from -0.4375 to 0.4375
- w_down: bfloat16 [768, 192], replicated, may hold values from -0.21875 to 0.21875
- vote_slot: int32 [131072], P(('grp', 'tile')), may hold values from 0 to 1023
- vote_owner: int32 [131072, 1], P(('grp', 'tile')), may hold values from 0 to 31; in each aligned block of 512 rows (0 to 511, 512 to 1023, ...) at most 32 rows name the same one
- vote_voxel: int32 [131072], P(('grp', 'tile')), may hold values from 0 to 255
Outputs:
- features_out: float32 [262144, 192], P(('grp', 'tile'))
- voxel_sums: float32 [65536, 192], P(('grp', 'tile'))
Inputs may be any that keep to these rules, and one draw needn't show every extreme that they name: `vote_owner`: among the votes of one shard, at most 32 name any one owner; some owner is named by exactly 32.
All inputs are finite; a program needn't handle non-finite values.
Results may differ from a plain program's by a relative error of at most 0.017.
Values may be sent and summed in bfloat16 or wider, within the bound.
A program may use at most 64 MiB of HBM per device.

v0:
```python
import jax
import jax.numpy as jnp
from jax import lax
from jax.sharding import PartitionSpec as P

HEADS = 12
WIN = 32
VOX_DEV = 256


def position(node_ids, pos_weight):
    rows = []
    for axis in range(3):
        total = jnp.zeros(node_ids.shape, jnp.int32)
        for level in range(6):
            bit = jnp.bitwise_and(jnp.right_shift(node_ids, 3 * level + axis), 1)
            total = total + bit * 2**level
        rows.append(total.astype(jnp.float32) / 64.0 - 0.5)
    coords = jnp.stack(rows, 0)
    return jnp.einsum("an,ac->nc", coords, pos_weight, precision=lax.Precision.HIGHEST)


def normed(x, gain):
    mean = jnp.mean(x, -1, keepdims=True)
    var = jnp.mean((x - mean) ** 2, -1, keepdims=True)
    return ((x - mean) * lax.rsqrt(var + 1e-05) * gain).astype(jnp.bfloat16)


def attend(windows, keep, gain, w_qkv, w_out):
    xf = windows.astype(jnp.float32)
    count, width, chans = windows.shape
    head_dim = chans // HEADS
    inner = normed(xf, gain)
    qkv = jnp.einsum("nwc,cd->nwd", inner, w_qkv, preferred_element_type=jnp.float32).astype(
        jnp.bfloat16
    )
    qkv = qkv.reshape(count, width, 3, HEADS, head_dim)
    query, keys, values = (qkv[:, :, 0], qkv[:, :, 1], qkv[:, :, 2])
    scores = jnp.einsum(
        "nqhd,nkhd->nhqk", query, keys, preferred_element_type=jnp.float32
    ) * head_dim ** (-0.5)
    scores = scores + ((keep - 1.0) * 1000000000.0)[:, None, None, :]
    probs = jax.nn.softmax(scores, -1).astype(jnp.bfloat16)
    context = jnp.einsum("nhqk,nkhd->nqhd", probs, values, preferred_element_type=jnp.float32)
    context = context.reshape(count, width, chans).astype(jnp.bfloat16)
    return xf + jnp.einsum("nwc,cd->nwd", context, w_out, preferred_element_type=jnp.float32)


def feed(x, gain, w_up, w_down):
    inner = normed(x, gain)
    hidden = jax.nn.gelu(
        jnp.einsum("nwc,cd->nwd", inner, w_up, preferred_element_type=jnp.float32)
    ).astype(jnp.bfloat16)
    return x + jnp.einsum("nwd,dc->nwc", hidden, w_down, preferred_element_type=jnp.float32)


def body(
    nodes,
    node_ids,
    node_count,
    pos_weight,
    gain_one,
    qkv_one,
    out_one,
    gain_two,
    qkv_two,
    out_two,
    gain_three,
    w_up,
    w_down,
    vote_slot,
    vote_owner,
    vote_voxel,
):
    n_local, width = nodes.shape
    groups = lax.axis_size("grp")
    block = n_local // groups
    run = WIN // groups
    keep = (jnp.arange(n_local, dtype=jnp.int32) < node_count[0]).astype(jnp.float32)
    start = (nodes.astype(jnp.float32) + position(node_ids, pos_weight)).astype(jnp.bfloat16)
    first = attend(
        start.reshape(n_local // WIN, WIN, width),
        keep.reshape(n_local // WIN, WIN),
        gain_one,
        qkv_one,
        out_one,
    )
    first = first.astype(jnp.bfloat16).reshape(groups, block, width)
    arrived, arrived_keep = (
        lax.all_to_all(first, "grp", split_axis=0, concat_axis=0, tiled=True),
        lax.all_to_all(
            keep.astype(jnp.bfloat16).reshape(groups, block),
            "grp",
            split_axis=0,
            concat_axis=0,
            tiled=True,
        ),
    )
    windows = (
        arrived.reshape(groups, block // run, run, width)
        .transpose(1, 0, 2, 3)
        .reshape(block // run, WIN, width)
    )
    window_keep = (
        arrived_keep.reshape(groups, block // run, run)
        .transpose(1, 0, 2)
        .reshape(block // run, WIN)
    )
    second = attend(windows, window_keep.astype(jnp.float32), gain_two, qkv_two, out_two)
    third = feed(second, gain_three, w_up, w_down)
    outgoing = (
        third.reshape(block // run, groups, run, width)
        .transpose(1, 0, 2, 3)
        .reshape(groups, block, width)
    )
    returned = (
        lax.all_to_all(
            outgoing.astype(jnp.bfloat16), "grp", split_axis=0, concat_axis=0, tiled=True
        )
        .astype(outgoing.dtype)
        .reshape(n_local, width)
    )
    features_out = returned * keep[:, None]
    picked = features_out[vote_slot].astype(jnp.bfloat16)
    owner = vote_owner[:, 0]
    tiles = lax.axis_size("tile")
    target = owner * VOX_DEV + vote_voxel
    onehot = (jnp.arange(tiles * VOX_DEV, dtype=jnp.int32)[:, None] == target[None, :]).astype(
        jnp.bfloat16
    )
    partial_sums = jnp.dot(onehot, picked, preferred_element_type=jnp.float32)
    voxel_sums = lax.psum_scatter(
        partial_sums.astype(jnp.bfloat16), "tile", scatter_dimension=0, tiled=True
    ).astype(jnp.float32)
    return (features_out, voxel_sums)


def solution(mesh):
    in_specs = (
        P(("grp", "tile"), None),
        P(("grp", "tile")),
        P(("grp", "tile")),
        P(),
        P(),
        P(),
        P(),
        P(),
        P(),
        P(),
        P(),
        P(),
        P(),
        P(("grp", "tile")),
        P(("grp", "tile"), None),
        P(("grp", "tile")),
    )
    out_specs = (P(("grp", "tile"), None), P(("grp", "tile"), None))
    return jax.shard_map(body, mesh=mesh, in_specs=in_specs, out_specs=out_specs, check_vma=False)
```

profile of v0, /device:TPU:1, one launch (start us, length us, event | category | flops | bytes accessed | tf_op | source)
XLA Modules:
  0.0 315.8 jit_solution(16546456182962039157)
XLA Ops:
  7.2 0.0 copy-start
  7.9 0.6 copy.103
  8.5 6.4 %all-to-all-start.1 = ((bf16[8,1,128]{2,1,0:T(2,128)(2,1)}), bf16[8,1,128]{2,1,0:T(2,128)(2,1)S(1)}, u32[]{:S(2)}, u32[]{:S(2)}) async-start(bf16[8,1,128]{2,1,0:T(2,128)(2,1)} %copy.103), calls=%async_computation.1 | async-start | bytes 8192 | tf_op jit(solution)/shard_map/all_to_all | solution.py:91
  14.9 0.7 multiply_add_fusion.10
  15.6 1.9 fusion.65
  17.5 0.3 copy.82
  17.8 0.1 multiply_reduce_fusion.2
  17.9 0.1 div.51
  18.0 0.1 rsqrt.31
  18.1 1.7 convolution_convert_fusion.1
  19.8 3.3 %copy.83 = bf16[32,32,576]{1,2,0:T(8,128)(2,1)} copy(bf16[32,32,576]{2,1,0:T(8,128)(2,1)S(1)} %convolution_convert_fusion.1) | data formatting | bytes 2359296 | tf_op jit(solution)/shard_map/convert_element_type | solution.py:34
  23.1 3.0 fusion.24
  26.2 5.2 %fusion.66 = (f32[32,12,32]{2,1,0:T(8,128)S(1)}, f32[32,12,32,32]{2,3,1,0:T(8,128)S(1)}) fusion(f32[32,12,32,32]{2,3,1,0:T(8,128)S(1)} %fusion.24, f32[32,32]{1,0:T(8,128)S(1)} %add_multiply_fusion), kind=kOutput, calls=%fused_computation.108 | output fusion | flops 2359327 | bytes 3198976 | tf_op jit(solution)/shard_map/sub | solution.py:43
  31.4 0.0 copy-start.2
  31.4 2.5 fusion.22
  33.9 0.0 copy-start.5
  33.9 0.6 fusion.27
  34.5 1.0 copy.89
  35.5 0.0 all-to-all-done.1
  35.5 5.0 %all-to-all-start = ((bf16[8,128,192]{1,2,0:T(8,128)(2,1)}), bf16[8,128,192]{1,2,0:T(8,128)(2,1)S(1)}, u32[]{:S(2)}, u32[]{:S(2)}) async-start(bf16[8,128,192]{1,2,0:T(8,128)(2,1)} %copy.89), calls=%async_computation | async-start | bytes 786432 | tf_op jit(solution)/shard_map/all_to_all | solution.py:90
  40.4 0.0 copy-done.5
  40.4 0.1 copy.105
  40.5 0.1 copy.106
  40.6 0.1 copy.107
  40.7 7.4 %all-to-all-done = bf16[8,128,192]{1,2,0:T(8,128)(2,1)S(1)} async-done(((bf16[8,128,192]{1,2,0:T(8,128)(2,1)}), bf16[8,128,192]{1,2,0:T(8,128)(2,1)S(1)}, u32[]{:S(2)}, u32[]{:S(2)}) %all-to-all-start) | async-done | bytes 393248 | tf_op jit(solution)/shard_map/all_to_all | solution.py:90
  48.1 0.4 copy.90
  48.5 0.1 convert_bitcast_fusion
  48.6 0.3 fusion.31
  48.9 0.1 copy.92
  49.0 0.1 copy.95
  49.1 0.4 multiply_reduce_fusion.1
  49.5 0.1 copy.96
  49.7 0.1 copy.98
  49.7 0.4 copy.91
  50.2 0.4 reshape.186
  50.5 0.1 copy.94
  50.6 0.7 convolution_convert_fusion
  51.4 3.3 %copy.99 = bf16[32,32,576]{1,2,0:T(8,128)(2,1)} copy(bf16[32,32,576]{2,1,0:T(8,128)(2,1)S(1)} %convolution_convert_fusion) | data formatting | bytes 2359296 | tf_op jit(solution)/shard_map/convert_element_type | solution.py:34
  54.7 3.0 fusion.23
  57.7 5.2 %fusion.67 = (f32[32,12,32]{2,1,0:T(8,128)S(1)}, f32[32,12,32,32]{2,3,1,0:T(8,128)S(1)}) fusion(f32[32,12,32,32]{2,3,1,0:T(8,128)S(1)} %fusion.23, f32[32,32]{1,0:T(8,128)S(1)} %copy.107), kind=kOutput, calls=%fused_computation.109 | output fusion | flops 2359327 | bytes 3198976 | tf_op jit(solution)/shard_map/sub | solution.py:43
  62.9 0.0 copy-start.3
  62.9 2.5 fusion.21
  65.5 0.0 copy-start.8
  65.5 0.0 copy-start.9
  65.5 0.0 copy-done.3
  65.5 0.7 fusion.68
  66.2 0.4 multiply_reduce_fusion
  66.7 0.0 copy-start.4
  66.7 0.0 copy-start.6
  66.7 1.5 fusion.28
  68.1 0.2 convert_element_type.189
  68.3 0.1 copy.110
  68.4 1.1 copy.111
  69.5 4.6 %all-to-all-start.2 = ((bf16[8,128,192]{1,2,0:T(8,128)(2,1)}), bf16[8,128,192]{1,2,0:T(8,128)(2,1)S(1)}, u32[]{:S(2)}, u32[]{:S(2)}) async-start(bf16[8,128,192]{1,2,0:T(8,128)(2,1)} %copy.111), calls=%async_computation.2 | async-start | bytes 786432 | tf_op jit(solution)/shard_map/all_to_all | solution.py:117
  74.1 0.0 reduce-scatter.2.cloned.1.call-start
  74.2 7.7 %all-to-all-done.2 = bf16[8,128,192]{1,2,0:T(8,128)(2,1)S(1)} async-done(((bf16[8,128,192]{1,2,0:T(8,128)(2,1)}), bf16[8,128,192]{1,2,0:T(8,128)(2,1)S(1)}, u32[]{:S(2)}, u32[]{:S(2)}) %all-to-all-start.2) | async-done | bytes 393248 | tf_op jit(solution)/shard_map/all_to_all | solution.py:117
  81.8 0.2 copy.112
  82.1 0.2 bitcast_multiply_fusion
  82.3 1.6 gather_fusion
  83.8 5.6 %fusion.3 = bf16[8192,192]{0,1:T(8,128)(2,1)} fusion(s32[512]{0:T(512)S(1)} %add.178, bf16[512,192]{1,0:T(8,128)(2,1)S(1)} %gather_fusion), kind=kOutput, calls=%fused_computation.5 | convolution fusion | flops 1616379904 | bytes 3344384 | tf_op jit(solution)/shard_map/dot_general | solution.py:131
  89.4 0.0 reduce-scatter.2.cloned.1.call-update
  89.4 1.2 copy.113
  90.6 216.7 %reduce-scatter.2.cloned.1.call-done = bf16[256,192]{0,1:T(8,128)(2,1)} async-done(((bf16[8192,192]{0,1:T(8,128)(2,1)}), bf16[256,192]{0,1:T(8,128)(2,1)}) %reduce-scatter.2.cloned.1.call-update) | async-done | bytes 98320 | tf_op jit(solution)/shard_map/reduce_scatter | solution.py:132
  307.3 1.6 convert_element_type.195
  (26 shorter events, 0.1 us)
Async XLA Ops:
  7.2 59.5 %copy-start = (bf16[768,192]{0,1:T(8,128)(2,1)S(1)}, bf16[768,192]{0,1:T(8,128)(2,1)}, u32[]{:S(2)}) copy-start(bf16[768,192]{0,1:T(8,128)(2,1)} %param.28) | copy-start | bytes 884740
  8.5 27.0 %all-to-all-start.1 = ((bf16[8,1,128]{2,1,0:T(2,128)(2,1)}), bf16[8,1,128]{2,1,0:T(2,128)(2,1)S(1)}, u32[]{:S(2)}, u32[]{:S(2)}) async-start(bf16[8,1,128]{2,1,0:T(2,128)(2,1)} %copy.103), calls=%async_computation.1 | async-start | bytes 8192 | tf_op jit(solution)/shard_map/all_to_all | solution.py:91
  31.4 2.5 copy-start.2
  33.9 6.5 %copy-start.5 = (s32[512,1]{0,1:T(1,128)S(1)}, s32[512,1]{0,1:T(1,128)}, u32[]{:S(2)}) copy-start(s32[512,1]{0,1:T(1,128)} %param.30) | copy-start | bytes 6148
  35.5 15.2 %copy-start.1 = (bf16[192,576]{1,0:T(8,128)(2,1)S(1)}, bf16[192,576]{1,0:T(8,128)(2,1)}, u32[]{:S(2)}) copy-start(bf16[192,576]{1,0:T(8,128)(2,1)} %param.24) | copy-start | bytes 663556
  35.5 15.2 %copy-start.7 = (f32[192]{0:T(256)S(1)}, f32[192]{0:T(256)}, u32[]{:S(2)}) copy-start(f32[192]{0:T(256)} %param.23) | copy-start | bytes 2308
  35.5 12.7 %all-to-all-start = ((bf16[8,128,192]{1,2,0:T(8,128)(2,1)}), bf16[8,128,192]{1,2,0:T(8,128)(2,1)S(1)}, u32[]{:S(2)}, u32[]{:S(2)}) async-start(bf16[8,128,192]{1,2,0:T(8,128)(2,1)} %copy.89), calls=%async_computation | async-start | bytes 786432 | tf_op jit(solution)/shard_map/all_to_all | solution.py:90
  62.9 2.6 copy-start.3
  65.5 1.2 copy-start.8
  65.5 1.2 copy-start.9
  66.7 7.5 %copy-start.4 = (s32[512]{0:T(512)S(1)}, s32[512]{0:T(512)}, u32[]{:S(2)}) copy-start(s32[512]{0:T(512)} %param.31) | copy-start | bytes 6148
  66.7 7.5 %copy-start.6 = (s32[512]{0:T(512)S(1)}, s32[512]{0:T(512)}, u32[]{:S(2)}) copy-start(s32[512]{0:T(512)} %param.29) | copy-start | bytes 6148
  69.5 12.3 %all-to-all-start.2 = ((bf16[8,128,192]{1,2,0:T(8,128)(2,1)}), bf16[8,128,192]{1,2,0:T(8,128)(2,1)S(1)}, u32[]{:S(2)}, u32[]{:S(2)}) async-start(bf16[8,128,192]{1,2,0:T(8,128)(2,1)} %copy.111), calls=%async_computation.2 | async-start | bytes 786432 | tf_op jit(solution)/shard_map/all_to_all | solution.py:117
  74.1 233.2 %reduce-scatter.2.cloned.1.call-start = ((), (), s32[]{:S(2)}) async-start(), calls=%async_computation.4 | async-start | bytes 3244032 | tf_op jit(solution)/shard_map/reduce_scatter | solution.py:132
Sparse Core Ops, SparseCore 0:
  89.6 217.7 reduce-scatter.1
where the time goes:
time: 321 us; the launch traced here: 316 us
  waiting for transfers between devices  232 us (72%)
  matrix products  23.8 us (7%)
  starting transfers between devices  15.9 us (5%)
  between operations  15.1 us (5%)
  local copies, waits for them, and re-layouts  14.9 us (5%)
  other arithmetic  14.2 us (4%)
    reduce_scatter x1, waiting for transfers between devices, body(): lax.psum_scatter(partial_sums.astype(jnp.bfloat16), 'tile', scatter_dimen...  217 us
    sub x2, other arithmetic, attend(): probs = jax.nn.softmax(scores, -1).astype(jnp.bfloat16)  10.4 us
    all_to_all x1, waiting for transfers between devices, body(): lax.all_to_all(outgoing.astype(jnp.bfloat16), 'grp', split_axis=0, concat...  7.66 us
    all_to_all x1, waiting for transfers between devices, body(): lax.all_to_all(first, 'grp', split_axis=0, concat_axis=0, tiled=True)  7.42 us
    convert_element_type x2, local copies, waits for them, and re-layouts, attend(): jnp.einsum('nwc,cd->nwd', inner, w_qkv, preferred_element_type=jnp.float32)  6.63 us
  transfers between devices with their start and end apart: 4, of which 3 were waited for; matrix products, arithmetic and copies ran while one was open for 7% of the time, Pallas kernels for 0%

commit v1 on v0

--- a/solution.py
+++ b/solution.py
@@ -6,6 +6,7 @@
 HEADS = 12
 WIN = 32
 VOX_DEV = 256
+CAP = 32
 
 
 def position(node_ids, pos_weight):
@@ -54,6 +55,22 @@
     return x + jnp.einsum("nwd,dc->nwc", hidden, w_down, preferred_element_type=jnp.float32)
 
 
+def pack_votes(owner, voxel):
+    tiles = lax.axis_size("tile")
+    votes = owner.shape[0]
+    named = (owner[:, None] == jnp.arange(tiles, dtype=jnp.int32)[None, :]).astype(jnp.bfloat16)
+    index = jnp.arange(votes, dtype=jnp.int32)
+    earlier = (index[None, :] < index[:, None]).astype(jnp.bfloat16)
+    rank = jnp.sum(jnp.dot(earlier, named, preferred_element_type=jnp.float32) * named, 1)
+    place = owner * CAP + rank.astype(jnp.int32)
+    packing = (jnp.arange(tiles * CAP, dtype=jnp.int32)[:, None] == place[None, :]).astype(jnp.bfloat16)
+    voxels = jnp.dot(packing, voxel.astype(jnp.bfloat16)[:, None], preferred_element_type=jnp.float32)
+    received = lax.all_to_all(
+        voxels.astype(jnp.bfloat16).reshape(tiles, CAP), "tile", split_axis=0, concat_axis=0, tiled=True
+    )
+    return packing, received.reshape(tiles * CAP).astype(jnp.int32)
+
+
 def body(
     nodes,
     node_ids,
@@ -73,6 +90,7 @@
     vote_voxel,
 ):
     n_local, width = nodes.shape
+    packing, voxel_of = pack_votes(vote_owner[:, 0], vote_voxel)
     groups = lax.axis_size("grp")
     block = n_local // groups
     run = WIN // groups
@@ -121,17 +139,18 @@
         .reshape(n_local, width)
     )
     features_out = returned * keep[:, None]
-    picked = features_out[vote_slot].astype(jnp.bfloat16)
-    owner = vote_owner[:, 0]
     tiles = lax.axis_size("tile")
-    target = owner * VOX_DEV + vote_voxel
-    onehot = (jnp.arange(tiles * VOX_DEV, dtype=jnp.int32)[:, None] == target[None, :]).astype(
-        jnp.bfloat16
-    )
-    partial_sums = jnp.dot(onehot, picked, preferred_element_type=jnp.float32)
-    voxel_sums = lax.psum_scatter(
-        partial_sums.astype(jnp.bfloat16), "tile", scatter_dimension=0, tiled=True
-    ).astype(jnp.float32)
+    received = lax.all_to_all(
+        jnp.dot(packing, features_out.astype(jnp.bfloat16)[vote_slot], preferred_element_type=jnp.float32)
+        .astype(jnp.bfloat16)
+        .reshape(tiles, CAP, width),
+        "tile",
+        split_axis=0,
+        concat_axis=0,
+        tiled=True,
+    ).reshape(tiles * CAP, width)
+    sums = (jnp.arange(VOX_DEV, dtype=jnp.int32)[:, None] == voxel_of[None, :]).astype(jnp.bfloat16)
+    voxel_sums = jnp.dot(sums, received, preferred_element_type=jnp.float32)
     return (features_out, voxel_sums)
 
 

time: 321 us -> 118 us (0.37)
  the two profiles are of different devices: /device:TPU:1 before, /device:TPU:32 now
where the time goes in v1:
time: 118 us; the launch traced here: 117 us
  waiting for transfers between devices  36 us (31%)
  starting transfers between devices  29.2 us (25%)
  matrix products  20.6 us (17%)
  local copies, waits for them, and re-layouts  17.1 us (14%)
  other arithmetic  12.7 us (11%)
  between operations  1.78 us (2%)
    all_to_all x1, waiting for transfers between devices, body(): lax.all_to_all(jnp.dot(packing, features_out.astype(jnp.bfloat16)[vote_sl...  15.2 us
    all_to_all x1, starting transfers between devices, pack_votes(): lax.all_to_all(voxels.astype(jnp.bfloat16).reshape(tiles, CAP), 'tile', s...  11.4 us
    sub x2, other arithmetic, attend(): probs = jax.nn.softmax(scores, -1).astype(jnp.bfloat16)  10.4 us
    all_to_all x1, waiting for transfers between devices, body(): lax.all_to_all(first, 'grp', split_axis=0, concat_axis=0, tiled=True)  8.17 us
    all_to_all x1, waiting for transfers between devices, body(): lax.all_to_all(outgoing.astype(jnp.bfloat16), 'grp', split_axis=0, concat...  8.11 us
    convert_element_type x2, local copies, waits for them, and re-layouts, attend(): jnp.einsum('nwc,cd->nwd', inner, w_qkv, preferred_element_type=jnp.float32)  6.63 us
    dot_general x2, matrix products, attend(): jnp.einsum('nqhd,nkhd->nhqk', query, keys, preferred_element_type=jnp.flo...  6.1 us
    all_to_all x1, starting transfers between devices, body(): lax.all_to_all(jnp.dot(packing, features_out.astype(jnp.bfloat16)[vote_sl...  5.24 us
  transfers between devices with their start and end apart: 5, of which 4 were waited for; matrix products, arithmetic and copies ran while one was open for 23% of the time, Pallas kernels for 0%

profile of v1, /device:TPU:32, one launch (start us, length us, event | category | flops | bytes accessed | tf_op | source)
XLA Modules:
  0.0 117.4 jit_solution(15805999621269917771)
XLA Ops:
  0.6 0.0 copy-start
  1.3 0.6 copy.106
  1.9 4.3 %all-to-all-start.1 = ((bf16[8,1,128]{2,1,0:T(2,128)(2,1)}), bf16[8,1,128]{2,1,0:T(2,128)(2,1)S(1)}, u32[]{:S(2)}, u32[]{:S(2)}) async-start(bf16[8,1,128]{2,1,0:T(2,128)(2,1)} %copy.106), calls=%async_computation.1 | async-start | bytes 8192 | tf_op jit(solution)/shard_map/all_to_all | solution.py:109
  6.2 0.7 multiply_add_fusion.10
  7.0 1.9 %fusion.72 = (f32[1024]{0:T(1024)S(1)}, f32[1024,192]{0,1:T(8,128)S(1)}) fusion(f32[3,192]{1,0:T(4,128)} %param.19, f32[1,1024]{1,0:T(1,128)S(1)} %bitcast.117, f32[1,1024]{1,0:T(1,128)S(1)} %bitcast.118, f32[1,1024]{1,0:T(1,128)S(1)} %bitcast.116, bf16[1024,192]{0,1:T(8,128)(2,1)} %param.16), kind=kOutput, calls=%fused_computation.119 | convolution fusion | flops 8066048 | bytes 1198336 | tf_op jit(solution)/shard_map/an,ac->nc/dot_general | solution.py:21
  8.8 0.3 copy.85
  9.2 0.1 multiply_reduce_fusion.2
  9.3 0.1 div.51
  9.4 0.1 rsqrt.31
  9.4 1.7 %convolution_convert_fusion.1 = bf16[32,32,576]{2,1,0:T(8,128)(2,1)S(1)} fusion(f32[32,32,192]{2,1,0:T(8,128)S(1)} %bitcast.103, f32[192]{0:T(256)} %param.20, f32[32,32]{1,0:T(8,128)S(1)} %rsqrt.31, f32[32,32]{1,0:T(8,128)S(1)} %div.51, bf16[192,576]{1,0:T(8,128)(2,1)} %param.21), kind=kOutput, calls=%fused_computation.32 | convolution fusion | flops 227868672 | bytes 2196224 | tf_op jit(solution)/shard_map/nwc,cd->nwd/dot_general | solution.py:35
  11.2 3.3 %copy.86 = bf16[32,32,576]{1,2,0:T(8,128)(2,1)} copy(bf16[32,32,576]{2,1,0:T(8,128)(2,1)S(1)} %convolution_convert_fusion.1) | data formatting | bytes 2359296 | tf_op jit(solution)/shard_map/convert_element_type | solution.py:35
  14.5 3.1 %fusion.23 = f32[32,12,32,32]{2,3,1,0:T(8,128)S(1)} fusion(bf16[32,32,3,12,16]{1,4,3,2,0:T(8,128)(2,1)} %bitcast.99), kind=kOutput, calls=%fused_computation.38 | convolution fusion | flops 12582912 | bytes 4718592 | tf_op jit(solution)/shard_map/nqhd,nkhd->nhqk/dot_general | solution.py:40
  17.6 0.3 fusion.31
  17.8 5.2 %fusion.73 = (f32[32,12,32]{2,1,0:T(8,128)S(1)}, f32[32,12,32,32]{2,3,1,0:T(8,128)S(1)}) fusion(f32[32,12,32,32]{2,3,1,0:T(8,128)S(1)} %fusion.23, f32[32,32]{1,0:T(8,128)S(1)} %add_multiply_fusion), kind=kOutput, calls=%fused_computation.120 | output fusion | flops 2359327 | bytes 3198976 | tf_op jit(solution)/shard_map/sub | solution.py:44
  23.0 0.0 copy-start.2
  23.0 0.0 copy-start.5
  23.0 2.5 %fusion.21 = bf16[32,12,16,32]{3,2,1,0:T(8,128)(2,1)S(1)} fusion(f32[32,12,32,32]{2,3,1,0:T(8,128)S(1)} %get-tuple-element.18, f32[32,12,32]{2,1,0:T(8,128)S(1)} %get-tuple-element.17, bf16[32,32,3,12,16]{1,4,3,2,0:T(8,128)(2,1)} %bitcast.100), kind=kOutput, calls=%fused_computation.30 | convolution fusion | flops 13565952 | bytes 3588096 | tf_op jit(solution)/shard_map/nhqk,nkhd->nqhd/dot_general | solution.py:45
  25.6 0.6 fusion.26
  26.2 1.0 copy.92
  27.1 4.8 %all-to-all-start = ((bf16[8,128,192]{1,2,0:T(8,128)(2,1)}), bf16[8,128,192]{1,2,0:T(8,128)(2,1)S(1)}, u32[]{:S(2)}, u32[]{:S(2)}) async-start(bf16[8,128,192]{1,2,0:T(8,128)(2,1)} %copy.92), calls=%async_computation | async-start | bytes 786432 | tf_op jit(solution)/shard_map/all_to_all | solution.py:108
  32.0 0.5 fusion.19
  32.4 0.1 copy.108
  32.5 0.1 copy.109
  32.6 0.1 copy.110
  32.7 8.2 %all-to-all-done = bf16[8,128,192]{1,2,0:T(8,128)(2,1)S(1)} async-done(((bf16[8,128,192]{1,2,0:T(8,128)(2,1)}), bf16[8,128,192]{1,2,0:T(8,128)(2,1)S(1)}, u32[]{:S(2)}, u32[]{:S(2)}) %all-to-all-start) | async-done | bytes 393248 | tf_op jit(solution)/shard_map/all_to_all | solution.py:108
  40.9 0.4 copy.93
  41.3 0.3 fusion.35
  41.5 0.1 copy.95
  41.6 0.1 copy.98
  41.7 0.1 convert_bitcast_fusion
  41.9 0.4 multiply_reduce_fusion.1
  42.3 0.1 copy.99
  42.4 0.1 copy.101
  42.5 0.1 copy.97
  42.6 0.4 copy.94
  43.0 0.4 reshape.218
  43.4 0.7 convolution_convert_fusion
  44.1 3.3 %copy.102 = bf16[32,32,576]{1,2,0:T(8,128)(2,1)} copy(bf16[32,32,576]{2,1,0:T(8,128)(2,1)S(1)} %convolution_convert_fusion) | data formatting | bytes 2359296 | tf_op jit(solution)/shard_map/convert_element_type | solution.py:35
  47.4 3.0 %fusion.22 = f32[32,12,32,32]{2,3,1,0:T(8,128)S(1)} fusion(bf16[32,32,3,12,16]{1,4,3,2,0:T(8,128)(2,1)} %bitcast.101), kind=kOutput, calls=%fused_computation.34 | convolution fusion | flops 12582912 | bytes 4718592 | tf_op jit(solution)/shard_map/nqhd,nkhd->nhqk/dot_general | solution.py:40
  50.5 5.2 %fusion.74 = (f32[32,12,32]{2,1,0:T(8,128)S(1)}, f32[32,12,32,32]{2,3,1,0:T(8,128)S(1)}) fusion(f32[32,12,32,32]{2,3,1,0:T(8,128)S(1)} %fusion.22, f32[32,32]{1,0:T(8,128)S(1)} %copy.110), kind=kOutput, calls=%fused_computation.121 | output fusion | flops 2359327 | bytes 3198976 | tf_op jit(solution)/shard_map/sub | solution.py:44
  55.7 2.5 %fusion.20 = bf16[32,12,16,32]{3,2,1,0:T(8,128)(2,1)S(1)} fusion(f32[32,12,32,32]{2,3,1,0:T(8,128)S(1)} %get-tuple-element.20, f32[32,12,32]{2,1,0:T(8,128)S(1)} %get-tuple-element.19, bf16[32,32,3,12,16]{1,4,3,2,0:T(8,128)(2,1)} %bitcast.102), kind=kOutput, calls=%fused_computation.29 | convolution fusion | flops 13565952 | bytes 3588096 | tf_op jit(solution)/shard_map/nhqk,nkhd->nqhd/dot_general | solution.py:45
  58.2 0.0 copy-start.8
  58.2 0.7 fusion.75
  59.0 0.4 multiply_reduce_fusion
  59.4 1.5 %fusion.27 = bf16[32,32,192]{2,1,0:T(8,128)(2,1)S(1)} fusion(f32[32,32,192]{2,1,0:T(8,128)S(1)} %get-tuple-element.22, f32[192]{0:T(256)S(1)} %copy-done.9, f32[32,32]{1,0:T(8,128)S(1)} %add_rsqrt_fusion, f32[32,32]{1,0:T(8,128)S(1)} %broadcast_multiply_fusion, bf16[768,192]{0,1:T(8,128)(2,1)S(1)} %copy-done, bf16[192,768]{1,0:T(8,128)(2,1)S(1)} %copy-done.8), kind=kOutput, calls=%fused_computation.46 | convolution fusion | flops 612237312 | bytes 1778432 | tf_op jit(solution)/shard_map/nwd,dc->nwc/dot_general | solution.py:55
  60.9 0.2 convert_element_type.218
  61.1 0.1 copy.113
  61.2 1.1 copy.114
  62.3 3.5 %all-to-all-start.2 = ((bf16[8,128,192]{1,2,0:T(8,128)(2,1)}), bf16[8,128,192]{1,2,0:T(8,128)(2,1)S(1)}, u32[]{:S(2)}, u32[]{:S(2)}) async-start(bf16[8,128,192]{1,2,0:T(8,128)(2,1)} %copy.114), calls=%async_computation.2 | async-start | bytes 786432 | tf_op jit(solution)/shard_map/all_to_all | solution.py:135
  65.8 0.7 all_to_all.25
  66.5 8.1 %all-to-all-done.2 = bf16[8,128,192]{1,2,0:T(8,128)(2,1)S(1)} async-done(((bf16[8,128,192]{1,2,0:T(8,128)(2,1)}), bf16[8,128,192]{1,2,0:T(8,128)(2,1)S(1)}, u32[]{:S(2)}, u32[]{:S(2)}) %all-to-all-start.2) | async-done | bytes 393248 | tf_op jit(solution)/shard_map/all_to_all | solution.py:135
  74.6 11.4 %all-to-all-start.3 = ((bf16[32,1,32]{2,1,0:T(2,128)(2,1)}), bf16[32,1,32]{2,1,0:T(2,128)(2,1)S(1)}, u32[]{:S(2)}, u32[]{:S(2)}) async-start(bf16[32,1,32]{2,1,0:T(2,128)(2,1)} %all_to_all.25), calls=%async_computation.3 | async-start | bytes 32768 | tf_op jit(solution)/shard_map/all_to_all | solution.py:68
  86.0 0.2 copy.115
  86.2 0.2 fusion.71
  86.4 2.0 %gather_fusion = bf16[512,192]{1,0:T(8,128)(2,1)S(1)} fusion(bf16[1024,192]{1,0:T(8,128)(2,1)S(1)} %get-tuple-element.10, s32[1024]{0:T(1024)S(1)} %pad_clamp_fusion), kind=kCustom, calls=%fused_computation | custom fusion | bytes 395264 | tf_op jit(solution)/shard_map/gather | solution.py:144
  88.4 0.6 fusion.28
  89.0 1.0 copy.117
  90.0 4.5 %all-to-all-done.3 = bf16[32,1,32]{2,1,0:T(2,128)(2,1)S(1)} async-done(((bf16[32,1,32]{2,1,0:T(2,128)(2,1)}), bf16[32,1,32]{2,1,0:T(2,128)(2,1)S(1)}, u32[]{:S(2)}, u32[]{:S(2)}) %all-to-all-start.3) | async-done | bytes 2080 | tf_op jit(solution)/shard_map/all_to_all | solution.py:68
  94.5 5.2 %all-to-all-start.4 = ((bf16[32,32,192]{2,1,0:T(8,128)(2,1)}), bf16[32,32,192]{2,1,0:T(8,128)(2,1)S(1)}, u32[]{:S(2)}, u32[]{:S(2)}) async-start(bf16[32,32,192]{2,1,0:T(8,128)(2,1)} %bitcast.37), calls=%async_computation.4 | async-start | bytes 1048576 | tf_op jit(solution)/shard_map/all_to_all | solution.py:143
  99.8 0.1 convert_reduce_fusion
  99.8 0.1 reshape.223
  99.9 1.2 %copy.118 = f32[1024,192]{0,1:T(8,128)} copy(f32[1024,192]{1,0:T(8,128)S(1)} %get-tuple-element.11) | data formatting | bytes 1572864
  101.1 15.2 %all-to-all-done.4 = bf16[32,32,192]{2,1,0:T(8,128)(2,1)S(1)} async-done(((bf16[32,32,192]{2,1,0:T(8,128)(2,1)}), bf16[32,32,192]{2,1,0:T(8,128)(2,1)S(1)}, u32[]{:S(2)}, u32[]{:S(2)}) %all-to-all-start.4) | async-done | bytes 393248 | tf_op jit(solution)/shard_map/all_to_all | solution.py:143
  116.3 1.1 fusion.34
  (35 shorter events, 0.2 us)
Async XLA Ops:
  0.6 58.8 %copy-start = (bf16[768,192]{0,1:T(8,128)(2,1)S(1)}, bf16[768,192]{0,1:T(8,128)(2,1)}, u32[]{:S(2)}) copy-start(bf16[768,192]{0,1:T(8,128)(2,1)} %param.28) | copy-start | bytes 884740
  1.9 25.2 %all-to-all-start.1 = ((bf16[8,1,128]{2,1,0:T(2,128)(2,1)}), bf16[8,1,128]{2,1,0:T(2,128)(2,1)S(1)}, u32[]{:S(2)}, u32[]{:S(2)}) async-start(bf16[8,1,128]{2,1,0:T(2,128)(2,1)} %copy.106), calls=%async_computation.1 | async-start | bytes 8192 | tf_op jit(solution)/shard_map/all_to_all | solution.py:109
  14.5 3.1 %copy-start.4 = (s32[512,1]{0,1:T(1,128)S(1)}, s32[512,1]{0,1:T(1,128)}, u32[]{:S(2)}) copy-start(s32[512,1]{0,1:T(1,128)} %param.30) | copy-start | bytes 6148
  23.0 2.5 %copy-start.2 = (bf16[192,192]{1,0:T(8,128)(2,1)S(1)}, bf16[192,192]{1,0:T(8,128)(2,1)}, u32[]{:S(2)}) copy-start(bf16[192,192]{1,0:T(8,128)(2,1)} %param.22) | copy-start | bytes 221188
  23.0 4.1 %copy-start.5 = (s32[512]{0:T(512)S(1)}, s32[512]{0:T(512)}, u32[]{:S(2)}) copy-start(s32[512]{0:T(512)} %param.31) | copy-start | bytes 6148
  27.1 13.7 %all-to-all-start = ((bf16[8,128,192]{1,2,0:T(8,128)(2,1)}), bf16[8,128,192]{1,2,0:T(8,128)(2,1)S(1)}, u32[]{:S(2)}, u32[]{:S(2)}) async-start(bf16[8,128,192]{1,2,0:T(8,128)(2,1)} %copy.92), calls=%async_computation | async-start | bytes 786432 | tf_op jit(solution)/shard_map/all_to_all | solution.py:108
  32.0 11.4 %copy-start.1 = (bf16[192,576]{1,0:T(8,128)(2,1)S(1)}, bf16[192,576]{1,0:T(8,128)(2,1)}, u32[]{:S(2)}) copy-start(bf16[192,576]{1,0:T(8,128)(2,1)} %param.24) | copy-start | bytes 663556
  32.0 11.4 %copy-start.7 = (f32[192]{0:T(256)S(1)}, f32[192]{0:T(256)}, u32[]{:S(2)}) copy-start(f32[192]{0:T(256)} %param.23) | copy-start | bytes 2308
  55.7 2.6 %copy-start.3 = (bf16[192,192]{1,0:T(8,128)(2,1)S(1)}, bf16[192,192]{1,0:T(8,128)(2,1)}, u32[]{:S(2)}) copy-start(bf16[192,192]{1,0:T(8,128)(2,1)} %param.25) | copy-start | bytes 221188
  58.2 1.2 %copy-start.8 = (bf16[192,768]{1,0:T(8,128)(2,1)S(1)}, bf16[192,768]{1,0:T(8,128)(2,1)}, u32[]{:S(2)}) copy-start(bf16[192,768]{1,0:T(8,128)(2,1)} %param.27) | copy-start | bytes 884740
  58.2 1.2 %copy-start.9 = (f32[192]{0:T(256)S(1)}, f32[192]{0:T(256)}, u32[]{:S(2)}) copy-start(f32[192]{0:T(256)} %param.26) | copy-start | bytes 2308
  59.4 7.0 %copy-start.6 = (s32[512]{0:T(512)S(1)}, s32[512]{0:T(512)}, u32[]{:S(2)}) copy-start(s32[512]{0:T(512)} %param.29) | copy-start | bytes 6148
  62.3 12.3 %all-to-all-start.2 = ((bf16[8,128,192]{1,2,0:T(8,128)(2,1)}), bf16[8,128,192]{1,2,0:T(8,128)(2,1)S(1)}, u32[]{:S(2)}, u32[]{:S(2)}) async-start(bf16[8,128,192]{1,2,0:T(8,128)(2,1)} %copy.114), calls=%async_computation.2 | async-start | bytes 786432 | tf_op jit(solution)/shard_map/all_to_all | solution.py:135
  74.6 19.9 %all-to-all-start.3 = ((bf16[32,1,32]{2,1,0:T(2,128)(2,1)}), bf16[32,1,32]{2,1,0:T(2,128)(2,1)S(1)}, u32[]{:S(2)}, u32[]{:S(2)}) async-start(bf16[32,1,32]{2,1,0:T(2,128)(2,1)} %all_to_all.25), calls=%async_computation.3 | async-start | bytes 32768 | tf_op jit(solution)/shard_map/all_to_all | solution.py:68
  94.5 21.8 %all-to-all-start.4 = ((bf16[32,32,192]{2,1,0:T(8,128)(2,1)}), bf16[32,32,192]{2,1,0:T(8,128)(2,1)S(1)}, u32[]{:S(2)}, u32[]{:S(2)}) async-start(bf16[32,32,192]{2,1,0:T(8,128)(2,1)} %bitcast.37), calls=%async_computation.4 | async-start | bytes 1048576 | tf_op jit(solution)/shard_map/all_to_all | solution.py:143

commit v2 on v0

v2 whole, which is shorter than its diff:
```python
import functools
import jax
import jax.numpy as jnp
from jax import lax
from jax.experimental import pallas as pl
from jax.experimental.pallas import tpu as pltpu
from jax.sharding import PartitionSpec as P

HEADS = 12
WIN = 32
VOX_DEV = 256
CAP = 32
LANES = 128
F32 = jnp.float32
BF16 = jnp.bfloat16
NT = (((1,), (1,)), ((), ()))
TN = (((0,), (0,)), ((), ()))
MESH = pl.DeviceIdType.MESH


def iota(shape, dim):
    return lax.broadcasted_iota(jnp.int32, shape, dim)


def mm(a, b, dims=(((1,), (0,)), ((), ()))):
    return lax.dot_general(a, b, dims, preferred_element_type=F32)


def normed(x, gain):
    mean = jnp.mean(x, -1, keepdims=True)
    var = jnp.mean((x - mean) ** 2, -1, keepdims=True)
    return ((x - mean) * lax.rsqrt(var + 1e-05) * gain).astype(BF16)


def attend(x, biases, gain, w_qv, w_k, w_out):
    chans = x.shape[1]
    dim = chans // HEADS
    inner = normed(x, gain)
    qv = mm(w_qv, inner, NT).astype(BF16)
    keys = mm(inner, w_k).astype(BF16)
    lane_win = iota((WIN, LANES), 1) // WIN
    own = [lane_win == w for w in range(LANES // WIN)]
    zero = jnp.zeros((WIN, LANES), BF16)
    halves = []
    for half, bias in enumerate(biases):
        lanes = slice(LANES * half, LANES * half + LANES)
        context = []
        for first in range(0, HEADS, 2):
            part = first * dim // LANES * LANES
            depth = min(LANES, chans - part)
            blocks = []
            for head in (first, first + 1):
                above = head * dim - part
                below = depth - above - dim
                pieces = [qv[head * dim : head * dim + dim, lanes]]
                if above:
                    pieces.insert(0, jnp.zeros((above, LANES), BF16))
                if below:
                    pieces.append(jnp.zeros((below, LANES), BF16))
                blocks.append(jnp.concatenate(pieces, 0))
            full = mm(keys[lanes, part : part + depth], jnp.concatenate(blocks, 1))
            probs, totals = [], []
            for i in range(2):
                wide = full[:, LANES * i : LANES * i + LANES]
                scores = wide[:WIN]
                for w in range(1, LANES // WIN):
                    scores = jnp.where(own[w], wide[WIN * w : WIN * w + WIN], scores)
                scores = scores + bias
                weights = jnp.exp(scores - jnp.max(scores, 0, keepdims=True))
                totals.append(jnp.sum(weights, 0, keepdims=True))
                weights = weights.astype(BF16)
                probs.append(jnp.concatenate([jnp.where(m, weights, zero) for m in own], 0))
            values = qv[chans + first * dim : chans + (first + 2) * dim, lanes]
            mixed = mm(values, jnp.concatenate(probs, 1))
            for i in range(2):
                piece = mixed[dim * i : dim * i + dim, LANES * i : LANES * i + LANES]
                context.append((piece / totals[i]).astype(BF16))
        halves.append(jnp.concatenate(context, 0))
    return x + mm(jnp.concatenate(halves, 1), w_out, TN)


def feed(x, gain, w_up, w_down):
    up = mm(normed(x, gain), w_up)
    inside = up * (0.7978845608028654 + 0.035677408136300125 * up * up)
    hidden = (0.5 * up * (1.0 + jnp.tanh(inside))).astype(BF16)
    return x + mm(hidden, w_down)


def turned(w, chans):
    dim = chans // HEADS
    eye = (iota((chans, chans), 0) == iota((chans, chans), 1)).astype(BF16)
    query = (mm(eye, w[:, :chans], NT) * dim**-0.5).astype(BF16)
    value = mm(eye, w[:, 2 * chans :], NT).astype(BF16)
    return jnp.concatenate([query, value], 0)


def columns(row):
    parts = []
    for t in range(row.shape[1] // LANES):
        piece = row[:, LANES * t : LANES * t + LANES].astype(F32)
        parts.append(jnp.broadcast_to(piece, (LANES, LANES)).T)
    return jnp.concatenate(parts, 0)


def place_positions(start, nodes, ids, pos_weight):
    groups, chunks, win, chans = start.shape
    row = iota((16, chans), 0)
    pick = [pos_weight[a : a + 1, :] for a in range(3)]
    spread = jnp.where(row % 3 == 0, pick[0], jnp.where(row % 3 == 1, pick[1], pick[2]))
    high = spread.astype(BF16).astype(F32)
    middle = (spread - high).astype(BF16).astype(F32)
    low = spread - high - middle
    split = jnp.where(row < 3, high, jnp.where(row < 6, middle, jnp.where(row < 9, low, 0.0))).astype(BF16)
    axes = []
    for axis in range(3):
        total = jnp.zeros(ids.shape, jnp.int32)
        for level in range(6):
            total = total + jnp.bitwise_and(jnp.right_shift(ids, 3 * level + axis), 1) * 2**level
        axes.append(total.astype(F32) / 64.0 - 0.5)
    slim = iota((16, LANES), 0)
    for g in range(groups):
        line = [a[g : g + 1, :] for a in axes]
        coords = jnp.where(slim % 3 == 0, line[0], jnp.where(slim % 3 == 1, line[1], line[2])).astype(BF16)
        moved = nodes[LANES * g : LANES * g + LANES, :].astype(F32) + mm(coords, split, TN)
        start[g] = moved.astype(BF16).reshape(chunks, win, chans)


def kernel(
    count_ref, nodes, ids, pos_weight, gain_one, qkv_one, out_one, gain_two, qkv_two, out_two,
    gain_three, w_up, w_down, slot_ref, owner_ref, voxel_ref,
    feat_out, vox_out,
    start, qv_one, qv_two, sent_one, got_one, sent_two, got_two, count_sent, count_got,
    vox_sent, vox_got, votes_sent, votes_got,
    count_ss, count_rs, vox_ss, vox_rs, one_ss, one_rs, two_ss, two_rs, vote_ss, vote_rs,
    *, groups, tiles,
):
    me, tile = lax.axis_index("grp"), lax.axis_index("tile")
    chans = nodes.shape[1]
    chunks = start.shape[1]
    block = chunks * WIN
    run = WIN // groups
    rows = groups * WIN
    count = count_ref[0]

    barrier = pltpu.get_barrier_semaphore()
    for d in range(1, groups):
        pl.semaphore_signal(barrier, inc=1, device_id=(lax.rem(me + d, groups), tile), device_id_type=MESH)
    for d in range(1, tiles):
        pl.semaphore_signal(barrier, inc=1, device_id=(me, lax.rem(tile + d, tiles)), device_id_type=MESH)

    def to_group(d, src, dst, ss, rs):
        return pltpu.make_async_remote_copy(
            src_ref=src, dst_ref=dst, send_sem=ss, recv_sem=rs,
            device_id=(lax.rem(me + d, groups), tile), device_id_type=MESH,
        )

    def to_tile(d, src, dst, ss, rs):
        return pltpu.make_async_remote_copy(
            src_ref=src, dst_ref=dst, send_sem=ss, recv_sem=rs,
            device_id=(me, lax.rem(tile + d, tiles)), device_id_type=MESH,
        )

    def count_copy(d):
        return to_group(d, count_sent, count_got.at[me], count_ss.at[d], count_rs.at[d])

    def vox_copy(d):
        peer = lax.rem(tile + d, tiles)
        return to_tile(d, vox_sent.at[peer], vox_got.at[tile], vox_ss.at[d], vox_rs.at[d])

    def one_copy(d, c):
        peer = lax.rem(me + d, groups)
        return to_group(d, sent_one.at[c, peer], got_one.at[c, me], one_ss.at[c, d], one_rs.at[c, d])

    def two_copy(d, c):
        peer = lax.rem(me + d, groups)
        return to_group(d, sent_two.at[c, peer], got_two.at[me, c], two_ss.at[c, d], two_rs.at[c, d])

    def vote_copy(d):
        peer = lax.rem(tile + d, tiles)
        return to_tile(d, votes_sent.at[peer], votes_got.at[tile], vote_ss.at[d], vote_rs.at[d])

    count_sent[...] = jnp.full(count_sent.shape, count, jnp.int32)
    count_got[me] = jnp.full(count_sent.shape, count, jnp.int32)
    place_positions(start, nodes, ids[...], pos_weight[...])
    qv_one[...] = turned(qkv_one[...], chans)
    qv_two[...] = turned(qkv_two[...], chans)

    votes = owner_ref.shape[1]
    owner = owner_ref[...].astype(F32)
    owner_col = columns(owner)
    earlier, later = iota((votes, LANES), 0), iota((votes, LANES), 1)
    ranks = []
    for t in range(votes // LANES):
        same = jnp.logical_and(owner_col == owner[:, LANES * t : LANES * t + LANES], earlier < later + LANES * t)
        ranks.append(jnp.sum(jnp.where(same, 1.0, 0.0), 0, keepdims=True))
    rank = jnp.concatenate(ranks, 1)
    place = owner * CAP + rank
    named = jnp.where(iota((tiles, votes), 0).astype(F32) == owner, voxel_ref[...].astype(F32), 0.0).astype(BF16)
    lane = iota((votes, LANES), 1)
    ranked = (columns(rank) == (lane % CAP).astype(F32)).astype(BF16)
    table = mm(named, ranked)
    share = LANES // CAP
    table = jnp.where(iota((tiles, LANES), 1) // CAP == lax.rem(tile, share), table, 0.0)
    for t in range(tiles):
        vox_sent[t] = jnp.broadcast_to(table[t : t + 1, :], vox_sent.shape[1:])
    vox_got[tile] = vox_sent[tile]

    pl.semaphore_wait(barrier, groups + tiles - 2)
    for d in range(1, groups):
        count_copy(d).start()
    for d in range(1, tiles):
        vox_copy(d).start()

    key = iota((WIN, LANES), 0)
    window = iota((WIN, LANES), 1) // WIN

    def stage_one(c, carry):
        x = jnp.concatenate([start[g, c] for g in range(groups)], 0).astype(F32)
        biases = []
        for half in range(rows // LANES):
            slot = (window + half * (LANES // WIN)) * block + c * WIN + key
            kept = jnp.where(slot < count, 1.0, 0.0)
            biases.append((kept - 1.0) * 1000000000.0)
        first = attend(x, biases, gain_one[...], qv_one[...], qkv_one[:, chans : 2 * chans], out_one[...])
        sent_one[c] = first.astype(BF16).reshape(groups, WIN, chans)
        got_one[c, me] = sent_one[c, me]
        for d in range(1, groups):
            one_copy(d, c).start()
        return carry

    lax.fori_loop(0, chunks, stage_one, 0)

    for d in range(1, groups):
        count_copy(d).wait_recv()
    counts = jnp.zeros((WIN, LANES), jnp.int32)
    for g in range(groups):
        counts = jnp.where(key // run == g, count_got[g][:1, :], counts)
    swap = (
        iota((rows, rows), 1)
        == iota((rows, rows), 0) // run % groups * WIN + iota((rows, rows), 0) // WIN * run + iota((rows, rows), 0) % run
    ).astype(BF16)

    def stage_two(c, carry):
        for d in range(1, groups):
            one_copy(d, c).wait_recv()
        x = mm(swap, got_one[c].reshape(rows, chans))
        biases = []
        for half in range(rows // LANES):
            slot = me * block + c * WIN + (half * (LANES // WIN) + window) * run + key % run
            kept = jnp.where(slot < counts, 1.0, 0.0)
            biases.append((kept - 1.0) * 1000000000.0)
        second = attend(x, biases, gain_two[...], qv_two[...], qkv_two[:, chans : 2 * chans], out_two[...])
        third = feed(second, gain_three[...], w_up[...], w_down[...])
        sent_two[c] = mm(swap, third.astype(BF16)).astype(BF16).reshape(groups, WIN, chans)
        got_two[me, c] = sent_two[c, me]
        for d in range(1, groups):
            two_copy(d, c).start()
        return carry

    lax.fori_loop(0, chunks, stage_two, 0)

    slots = nodes.shape[0]
    slot_col = columns(slot_ref[...])
    chosen = jnp.concatenate(
        [(slot_col == (lane + LANES * t).astype(F32)).astype(BF16) for t in range(slots // LANES)], 1
    )
    for d in range(1, tiles):
        vox_copy(d).wait_recv()
    vox = iota((VOX_DEV, LANES), 0).astype(F32)
    sums = []
    for a in range(tiles // share):
        mine = vox_got[share * a]
        for u in range(1, share):
            mine = mine + vox_got[share * a + u]
        sums.append((vox == mine[:1, :]).astype(BF16))
    sums = jnp.concatenate(sums, 1)

    for c in range(chunks):
        for d in range(1, groups):
            two_copy(d, c).wait_recv()
    back = got_two[...].reshape(slots, chans)
    feat = jnp.where(iota((slots, chans), 0) < count, back.astype(F32), 0.0).astype(BF16)
    feat_out[...] = feat
    picked = mm(chosen, feat).astype(BF16)
    packing = (iota((tiles * CAP, votes), 0).astype(F32) == place).astype(BF16)
    votes_sent[...] = mm(packing, picked).astype(BF16).reshape(tiles, CAP, chans)
    votes_got[tile] = votes_sent[tile]
    for d in range(1, tiles):
        vote_copy(d).start()
    for d in range(1, tiles):
        vote_copy(d).wait_recv()
    vox_out[...] = mm(sums, votes_got[...].reshape(tiles * CAP, chans))

    for d in range(1, groups):
        count_copy(d).wait_send()
        for c in range(chunks):
            one_copy(d, c).wait_send()
            two_copy(d, c).wait_send()
    for d in range(1, tiles):
        vox_copy(d).wait_send()
        vote_copy(d).wait_send()


def body(
    nodes, node_ids, node_count, pos_weight, gain_one, qkv_one, out_one, gain_two, qkv_two, out_two,
    gain_three, w_up, w_down, vote_slot, vote_owner, vote_voxel,
):
    slots, chans = nodes.shape
    votes = vote_slot.shape[0]
    groups, tiles = lax.axis_size("grp"), lax.axis_size("tile")
    chunks = slots // groups // WIN
    vmem = pl.BlockSpec(memory_space=pltpu.VMEM)
    dma = pltpu.SemaphoreType.DMA


    feat, sums = pl.pallas_call(
        functools.partial(kernel, groups=groups, tiles=tiles),
        out_shape=(
            jax.ShapeDtypeStruct((slots, chans), BF16),
            jax.ShapeDtypeStruct((VOX_DEV, chans), F32),
        ),
        in_specs=[pl.BlockSpec(memory_space=pltpu.SMEM)] + [vmem] * 15,
        out_specs=(vmem, vmem),
        scratch_shapes=[
            pltpu.VMEM((groups, chunks, WIN, chans), BF16),
            pltpu.VMEM((2 * chans, chans), BF16),
            pltpu.VMEM((2 * chans, chans), BF16),
            pltpu.VMEM((chunks, groups, WIN, chans), BF16),
            pltpu.VMEM((chunks, groups, WIN, chans), BF16),
            pltpu.VMEM((chunks, groups, WIN, chans), BF16),
            pltpu.VMEM((groups, chunks, WIN, chans), BF16),
            pltpu.VMEM((8, LANES), jnp.int32),
            pltpu.VMEM((groups, 8, LANES), jnp.int32),
            pltpu.VMEM((tiles, 8, LANES), F32),
            pltpu.VMEM((tiles, 8, LANES), F32),
            pltpu.VMEM((tiles, CAP, chans), BF16),
            pltpu.VMEM((tiles, CAP, chans), BF16),
            dma((groups,)), dma((groups,)), dma((tiles,)), dma((tiles,)),
            dma((chunks, groups)), dma((chunks, groups)), dma((chunks, groups)), dma((chunks, groups)),
            dma((tiles,)), dma((tiles,)),
        ],
        compiler_params=pltpu.CompilerParams(collective_id=0, has_side_effects=True),
    )(
        node_count, nodes, node_ids.reshape(slots // LANES, LANES), pos_weight,
        gain_one.reshape(1, chans), qkv_one, out_one, gain_two.reshape(1, chans), qkv_two, out_two,
        gain_three.reshape(1, chans), w_up, w_down,
        vote_slot.reshape(1, votes), vote_owner.reshape(1, votes), vote_voxel.reshape(1, votes),
    )
    return feat.astype(F32), sums


def solution(mesh):
    in_specs = (
        P(("grp", "tile"), None),
        P(("grp", "tile")),
        P(("grp", "tile")),
        P(),
        P(),
        P(),
        P(),
        P(),
        P(),
        P(),
        P(),
        P(),
        P(),
        P(("grp", "tile")),
        P(("grp", "tile"), None),
        P(("grp", "tile")),
    )
    out_specs = (P(("grp", "tile"), None), P(("grp", "tile"), None))
    return jax.shard_map(body, mesh=mesh, in_specs=in_specs, out_specs=out_specs, check_vma=False)
```

time: 321 us -> 70 us (0.22); the launches traced: 316 us -> 69.7 us
  waiting for transfers between devices: 232 us -> 0 us
  Pallas kernels: 0 us -> 61.7 us
  matrix products: 23.8 us -> 0 us
  starting transfers between devices: 15.9 us -> 0 us
  other arithmetic: 14.2 us -> 0 us
  between operations: 15.1 us -> 1.34 us
  local copies, waits for them, and re-layouts: 14.9 us -> 6.73 us
    reduce_scatter x1 -> x0, waiting for transfers between devices: 217 us -> none  [body(): lax.psum_scatter(partial_sums.astype(jnp.bfloat16), 'tile', scatter_dimen...]
    pallas_call x0 -> x1, Pallas kernels: none -> 61.7 us  [body(): pl.pallas_call(functools.partial(kernel, groups=groups, tiles=tiles), out...]
    dot_general x11 -> x0, matrix products: 23.8 us -> none  [the longest x2 6.09 us: attend(): jnp.einsum('nqhd,nkhd->nhqk', query, keys, preferred_element_type=jnp.flo...]
    all_to_all x3 -> x0, starting transfers between devices: 15.9 us -> none  [the longest x1 6.41 us: body(): lax.all_to_all(keep.astype(jnp.bfloat16).reshape(groups, block), 'grp', s...]
    all_to_all x3 -> x0, waiting for transfers between devices: 15.1 us -> none  [the longest x1 7.66 us: body(): lax.all_to_all(outgoing.astype(jnp.bfloat16), 'grp', split_axis=0, concat...]
    sub x3 -> x0, other arithmetic: 11.1 us -> none  [the longest x2 10.4 us: attend(): probs = jax.nn.softmax(scores, -1).astype(jnp.bfloat16)]
    convert_element_type x9 -> x0, local copies, waits for them, and re-layouts: 9.73 us -> none  [the longest x2 6.63 us: attend(): jnp.einsum('nwc,cd->nwd', inner, w_qkv, preferred_element_type=jnp.float32)]
    unnamed x21 -> x6, local copies, waits for them, and re-layouts: 1.26 us -> 6.73 us
  transfers between devices with their start and end apart: 4 -> 0, of which waited for: 3 -> 0; matrix products, arithmetic and copies ran while one was open for 7% -> 0% of each run, Pallas kernels for 0% -> 0%
where the time goes in v2:
time: 70 us; the launch traced here: 69.7 us
  Pallas kernels  61.7 us (88%)
  local copies, waits for them, and re-layouts  6.73 us (10%)
  between operations  1.34 us (2%)
    pallas_call x1, Pallas kernels, body(): pl.pallas_call(functools.partial(kernel, groups=groups, tiles=tiles), out...  61.7 us
    unnamed x6, local copies, waits for them, and re-layouts  6.73 us

profile of v2, /device:TPU:1, one launch (start us, length us, event | category | flops | bytes accessed | tf_op | source)
XLA Modules:
  0.0 69.7 jit_solution(17997256049364432739)
XLA Ops:
  0.6 0.0 copy-start
  1.3 1.9 %copy.19.w_down = bf16[768,192]{1,0:T(8,128)(2,1)} copy(bf16[768,192]{0,1:T(8,128)(2,1)} %param.28) | data formatting | bytes 589824 | tf_op args[12]
  3.2 0.0 copy-done
  3.2 1.0 %copy.18.nodes = bf16[1024,192]{1,0:T(8,128)(2,1)} copy(bf16[1024,192]{0,1:T(8,128)(2,1)S(1)} %copy-done) | data formatting | bytes 786432 | tf_op args[0]
  4.2 61.7 %shard_map.167 = (bf16[1024,192]{1,0:T(8,128)(2,1)}, f32[256,192]{1,0:T(8,128)}) custom-call(s32[1]{0:T(128)S(6)} %copy.22.count_ref, bf16[1024,192]{1,0:T(8,128)(2,1)} %copy.18.nodes, s32[8,128]{1,0:T(8,128)} %bitcast.7, f32[3,192]{1,0:T(4,128)} %pos_weight.1, f32[1,192]{1,0:T(1,128)} %bitcast.11, bf16[192,576]{1,0:T(8,128)(2,1)} %qkv_one.1, ...), custom_call_target="tpu_custom_call" | custom-call | tf_op jit(solution)/shard_map/pallas_call | solution.py:316
  65.9 1.7 %copy.21 = f32[256,192]{0,1:T(8,128)} copy(f32[256,192]{1,0:T(8,128)} %get-tuple-element.7) | data formatting | bytes 393216
  67.6 2.1 %copy.20 = f32[1024,192]{0,1:T(8,128)} copy(bf16[1024,192]{1,0:T(8,128)(2,1)} %get-tuple-element.4) | data formatting | bytes 1179648
Async XLA Ops:
  0.6 2.6 %copy-start = (bf16[1024,192]{0,1:T(8,128)(2,1)S(1)}, bf16[1024,192]{0,1:T(8,128)(2,1)}, u32[]{:S(2)}) copy-start(bf16[1024,192]{0,1:T(8,128)(2,1)} %param.16) | copy-start | bytes 1179652

commit v3 on v2

--- a/solution.py
+++ b/solution.py
@@ -16,6 +16,7 @@
 NT = (((1,), (1,)), ((), ()))
 TN = (((0,), (0,)), ((), ()))
 MESH = pl.DeviceIdType.MESH
+LOG2E = 1.4426950408889634
 
 
 def iota(shape, dim):
@@ -27,71 +28,90 @@
 
 
 def normed(x, gain):
-    mean = jnp.mean(x, -1, keepdims=True)
-    var = jnp.mean((x - mean) ** 2, -1, keepdims=True)
-    return ((x - mean) * lax.rsqrt(var + 1e-05) * gain).astype(BF16)
-
-
-def attend(x, biases, gain, w_qv, w_k, w_out):
-    chans = x.shape[1]
+    mean = jnp.mean(x, 0, keepdims=True)
+    var = jnp.mean((x - mean) ** 2, 0, keepdims=True)
+    return ((x - mean) * lax.rsqrt(var + 1e-05) * jnp.concatenate([gain] * (x.shape[1] // LANES), 1)).astype(BF16)
+
+
+def attend(x, biases, gain, w_qkv, w_out):
+    chans = x.shape[0]
     dim = chans // HEADS
-    inner = normed(x, gain)
-    qv = mm(w_qv, inner, NT).astype(BF16)
-    keys = mm(inner, w_k).astype(BF16)
+    wins = LANES // WIN
+    qkv = mm(w_qkv, normed(x, gain))
+    query = (qkv[:chans] * (dim**-0.5 * LOG2E)).astype(BF16)
+    keys = qkv[chans : 2 * chans].astype(BF16)
+    values = qkv[2 * chans :].astype(BF16)
     lane_win = iota((WIN, LANES), 1) // WIN
-    own = [lane_win == w for w in range(LANES // WIN)]
-    zero = jnp.zeros((WIN, LANES), BF16)
-    halves = []
-    for half, bias in enumerate(biases):
+    own = [lane_win == w for w in range(wins)]
+    own_short = [m[:dim] for m in own]
+    zero = jnp.zeros((dim, LANES), BF16)
+    pairs = [(half, first) for half in range(len(biases)) for first in range(0, HEADS, 2)]
+    scores = {}
+    for half, first in pairs:
         lanes = slice(LANES * half, LANES * half + LANES)
-        context = []
-        for first in range(0, HEADS, 2):
-            part = first * dim // LANES * LANES
-            depth = min(LANES, chans - part)
-            blocks = []
-            for head in (first, first + 1):
-                above = head * dim - part
-                below = depth - above - dim
-                pieces = [qv[head * dim : head * dim + dim, lanes]]
-                if above:
-                    pieces.insert(0, jnp.zeros((above, LANES), BF16))
-                if below:
-                    pieces.append(jnp.zeros((below, LANES), BF16))
-                blocks.append(jnp.concatenate(pieces, 0))
-            full = mm(keys[lanes, part : part + depth], jnp.concatenate(blocks, 1))
-            probs, totals = [], []
-            for i in range(2):
-                wide = full[:, LANES * i : LANES * i + LANES]
-                scores = wide[:WIN]
-                for w in range(1, LANES // WIN):
-                    scores = jnp.where(own[w], wide[WIN * w : WIN * w + WIN], scores)
-                scores = scores + bias
-                weights = jnp.exp(scores - jnp.max(scores, 0, keepdims=True))
-                totals.append(jnp.sum(weights, 0, keepdims=True))
-                weights = weights.astype(BF16)
-                probs.append(jnp.concatenate([jnp.where(m, weights, zero) for m in own], 0))
-            values = qv[chans + first * dim : chans + (first + 2) * dim, lanes]
-            mixed = mm(values, jnp.concatenate(probs, 1))
-            for i in range(2):
-                piece = mixed[dim * i : dim * i + dim, LANES * i : LANES * i + LANES]
-                context.append((piece / totals[i]).astype(BF16))
-        halves.append(jnp.concatenate(context, 0))
-    return x + mm(jnp.concatenate(halves, 1), w_out, TN)
+        rows = slice(first * dim, first * dim + 2 * dim)
+        two = query[rows, lanes]
+        blocks = jnp.concatenate(
+            [jnp.concatenate([two[:dim], zero], 1), jnp.concatenate([zero, two[dim:]], 1)], 0
+        )
+        full = mm(keys[rows, lanes], blocks, TN)
+        for i in range(2):
+            wide = full[:, LANES * i : LANES * i + LANES]
+            picked = wide[:WIN]
+            for w in range(1, wins):
+                picked = jnp.where(own[w], wide[WIN * w : WIN * w + WIN], picked)
+            scores[half, first + i] = picked + biases[half]
+    probs, totals = {}, {}
+    for key, score in scores.items():
+        weights = jnp.exp2(score - jnp.max(score, 0, keepdims=True))
+        totals[key] = 1.0 / jnp.sum(weights, 0, keepdims=True)
+        probs[key] = weights.astype(BF16)
+    context = {}
+    for half, first in pairs:
+        rows = slice(first * dim, first * dim + 2 * dim)
+        stacked = jnp.concatenate(
+            [values[rows, LANES * half + WIN * w : LANES * half + WIN * w + WIN] for w in range(wins)], 0
+        )
+        mixed = mm(stacked, jnp.concatenate([probs[half, first], probs[half, first + 1]], 1))
+        for i in range(2):
+            wide = mixed[:, LANES * i : LANES * i + LANES]
+            at = [2 * dim * w + dim * i for w in range(wins)]
+            picked = wide[at[0] : at[0] + dim]
+            for w in range(1, wins):
+                picked = jnp.where(own_short[w], wide[at[w] : at[w] + dim], picked)
+            context[half, first + i] = (picked * totals[half, first + i]).astype(BF16)
+    merged = jnp.concatenate(
+        [jnp.concatenate([context[half, h] for h in range(HEADS)], 0) for half in range(len(biases))], 1
+    )
+    return x + mm(w_out, merged)
 
 
 def feed(x, gain, w_up, w_down):
-    up = mm(normed(x, gain), w_up)
+    up = mm(w_up, normed(x, gain))
     inside = up * (0.7978845608028654 + 0.035677408136300125 * up * up)
     hidden = (0.5 * up * (1.0 + jnp.tanh(inside))).astype(BF16)
-    return x + mm(hidden, w_down)
-
-
-def turned(w, chans):
-    dim = chans // HEADS
-    eye = (iota((chans, chans), 0) == iota((chans, chans), 1)).astype(BF16)
-    query = (mm(eye, w[:, :chans], NT) * dim**-0.5).astype(BF16)
-    value = mm(eye, w[:, 2 * chans :], NT).astype(BF16)
-    return jnp.concatenate([query, value], 0)
+    return x + mm(w_down, hidden)
+
+
+def swapped(x, groups):
+    half = x.shape[0] // groups // 2
+    run = WIN // groups
+    parts = x.reshape(groups // 2, 2, groups // 2, 2 * run, x.shape[1])
+    low = iota((2 * run, x.shape[1]), 0) < run
+    out = []
+    for b in range(groups // 2):
+        for odd in range(2):
+            for a in range(groups // 2):
+                first, second = parts[a, 0, b], parts[a, 1, b]
+                if odd:
+                    out.append(jnp.where(low, pltpu.roll(first, run, 0), second))
+                else:
+                    out.append(jnp.where(low, first, pltpu.roll(second, run, 0)))
+    return jnp.concatenate(out, 0)
+
+
+def turned(w):
+    return w.astype(F32).T.astype(BF16)
 
 
 def columns(row):
@@ -121,21 +141,21 @@
     for g in range(groups):
         line = [a[g : g + 1, :] for a in axes]
         coords = jnp.where(slim % 3 == 0, line[0], jnp.where(slim % 3 == 1, line[1], line[2])).astype(BF16)
-        moved = nodes[LANES * g : LANES * g + LANES, :].astype(F32) + mm(coords, split, TN)
-        start[g] = moved.astype(BF16).reshape(chunks, win, chans)
+        moved = nodes[:, LANES * g : LANES * g + LANES].astype(F32) + mm(split, coords, TN)
+        start[g] = moved.T.astype(BF16).reshape(chunks, win, chans)
 
 
 def kernel(
     count_ref, nodes, ids, pos_weight, gain_one, qkv_one, out_one, gain_two, qkv_two, out_two,
     gain_three, w_up, w_down, slot_ref, owner_ref, voxel_ref,
     feat_out, vox_out,
-    start, qv_one, qv_two, sent_one, got_one, sent_two, got_two, count_sent, count_got,
+    start, in_one, proj_one, in_two, proj_two, up_turned, norm_one, norm_two, norm_three, sent_one, got_one, sent_two, got_two, count_sent, count_got,
     vox_sent, vox_got, votes_sent, votes_got,
     count_ss, count_rs, vox_ss, vox_rs, one_ss, one_rs, two_ss, two_rs, vote_ss, vote_rs,
     *, groups, tiles,
 ):
     me, tile = lax.axis_index("grp"), lax.axis_index("tile")
-    chans = nodes.shape[1]
+    chans = nodes.shape[0]
     chunks = start.shape[1]
     block = chunks * WIN
     run = WIN // groups
@@ -182,8 +202,13 @@
     count_sent[...] = jnp.full(count_sent.shape, count, jnp.int32)
     count_got[me] = jnp.full(count_sent.shape, count, jnp.int32)
     place_positions(start, nodes, ids[...], pos_weight[...])
-    qv_one[...] = turned(qkv_one[...], chans)
-    qv_two[...] = turned(qkv_two[...], chans)
+    in_one[...] = turned(qkv_one[...])
+    in_two[...] = turned(qkv_two[...])
+    proj_one[...] = turned(out_one[...])
+    proj_two[...] = turned(out_two[...])
+    up_turned[...] = turned(w_up[...])
+    for norm, gain in ((norm_one, gain_one), (norm_two, gain_two), (norm_three, gain_three)):
+        norm[...] = jnp.broadcast_to(gain[...], (LANES, chans)).T
 
     votes = owner_ref.shape[1]
     owner = owner_ref[...].astype(F32)
@@ -221,8 +246,8 @@
             slot = (window + half * (LANES // WIN)) * block + c * WIN + key
             kept = jnp.where(slot < count, 1.0, 0.0)
             biases.append((kept - 1.0) * 1000000000.0)
-        first = attend(x, biases, gain_one[...], qv_one[...], qkv_one[:, chans : 2 * chans], out_one[...])
-        sent_one[c] = first.astype(BF16).reshape(groups, WIN, chans)
+        first = attend(x.T, biases, norm_one[...], in_one[...], proj_one[...])
+        sent_one[c] = first.T.astype(BF16).reshape(groups, WIN, chans)
         got_one[c, me] = sent_one[c, me]
         for d in range(1, groups):
             one_copy(d, c).start()
@@ -235,23 +260,18 @@
     counts = jnp.zeros((WIN, LANES), jnp.int32)
     for g in range(groups):
         counts = jnp.where(key // run == g, count_got[g][:1, :], counts)
-    swap = (
-        iota((rows, rows), 1)
-        == iota((rows, rows), 0) // run % groups * WIN + iota((rows, rows), 0) // WIN * run + iota((rows, rows), 0) % run
-    ).astype(BF16)
-
     def stage_two(c, carry):
         for d in range(1, groups):
             one_copy(d, c).wait_recv()
-        x = mm(swap, got_one[c].reshape(rows, chans))
+        x = swapped(got_one[c].reshape(rows, chans).astype(F32), groups).T
         biases = []
         for half in range(rows // LANES):
             slot = me * block + c * WIN + (half * (LANES // WIN) + window) * run + key % run
             kept = jnp.where(slot < counts, 1.0, 0.0)
             biases.append((kept - 1.0) * 1000000000.0)
-        second = attend(x, biases, gain_two[...], qv_two[...], qkv_two[:, chans : 2 * chans], out_two[...])
-        third = feed(second, gain_three[...], w_up[...], w_down[...])
-        sent_two[c] = mm(swap, third.astype(BF16)).astype(BF16).reshape(groups, WIN, chans)
+        second = attend(x, biases, norm_two[...], in_two[...], proj_two[...])
+        third = feed(second, norm_three[...], up_turned[...], w_down[...])
+        sent_two[c] = swapped(third.T, groups).astype(BF16).reshape(groups, WIN, chans)
         got_two[me, c] = sent_two[c, me]
         for d in range(1, groups):
             two_copy(d, c).start()
@@ -259,7 +279,7 @@
 
     lax.fori_loop(0, chunks, stage_two, 0)
 
-    slots = nodes.shape[0]
+    slots = nodes.shape[1]
     slot_col = columns(slot_ref[...])
     chosen = jnp.concatenate(
         [(slot_col == (lane + LANES * t).astype(F32)).astype(BF16) for t in range(slots // LANES)], 1
@@ -280,7 +300,7 @@
             two_copy(d, c).wait_recv()
     back = got_two[...].reshape(slots, chans)
     feat = jnp.where(iota((slots, chans), 0) < count, back.astype(F32), 0.0).astype(BF16)
-    feat_out[...] = feat
+    feat_out[...] = feat.astype(F32).T.astype(BF16)
     picked = mm(chosen, feat).astype(BF16)
     packing = (iota((tiles * CAP, votes), 0).astype(F32) == place).astype(BF16)
     votes_sent[...] = mm(packing, picked).astype(BF16).reshape(tiles, CAP, chans)
@@ -289,7 +309,7 @@
         vote_copy(d).start()
     for d in range(1, tiles):
         vote_copy(d).wait_recv()
-    vox_out[...] = mm(sums, votes_got[...].reshape(tiles * CAP, chans))
+    vox_out[...] = mm(sums, votes_got[...].reshape(tiles * CAP, chans)).T
 
     for d in range(1, groups):
         count_copy(d).wait_send()
@@ -316,15 +336,21 @@
     feat, sums = pl.pallas_call(
         functools.partial(kernel, groups=groups, tiles=tiles),
         out_shape=(
-            jax.ShapeDtypeStruct((slots, chans), BF16),
-            jax.ShapeDtypeStruct((VOX_DEV, chans), F32),
+            jax.ShapeDtypeStruct((chans, slots), BF16),
+            jax.ShapeDtypeStruct((chans, VOX_DEV), F32),
         ),
         in_specs=[pl.BlockSpec(memory_space=pltpu.SMEM)] + [vmem] * 15,
         out_specs=(vmem, vmem),
         scratch_shapes=[
             pltpu.VMEM((groups, chunks, WIN, chans), BF16),
-            pltpu.VMEM((2 * chans, chans), BF16),
-            pltpu.VMEM((2 * chans, chans), BF16),
+            pltpu.VMEM((3 * chans, chans), BF16),
+            pltpu.VMEM((chans, chans), BF16),
+            pltpu.VMEM((3 * chans, chans), BF16),
+            pltpu.VMEM((chans, chans), BF16),
+            pltpu.VMEM((w_up.shape[1], chans), BF16),
+            pltpu.VMEM((chans, LANES), F32),
+            pltpu.VMEM((chans, LANES), F32),
+            pltpu.VMEM((chans, LANES), F32),
             pltpu.VMEM((chunks, groups, WIN, chans), BF16),
             pltpu.VMEM((chunks, groups, WIN, chans), BF16),
             pltpu.VMEM((chunks, groups, WIN, chans), BF16),
@@ -341,12 +367,12 @@
         ],
         compiler_params=pltpu.CompilerParams(collective_id=0, has_side_effects=True),
     )(
-        node_count, nodes, node_ids.reshape(slots // LANES, LANES), pos_weight,
+        node_count, nodes.T, node_ids.reshape(slots // LANES, LANES), pos_weight,
         gain_one.reshape(1, chans), qkv_one, out_one, gain_two.reshape(1, chans), qkv_two, out_two,
-        gain_three.reshape(1, chans), w_up, w_down,
+        gain_three.reshape(1, chans), w_up, w_down.T,
         vote_slot.reshape(1, votes), vote_owner.reshape(1, votes), vote_voxel.reshape(1, votes),
     )
-    return feat.astype(F32), sums
+    return feat.T.astype(F32), sums.T
 
 
 def solution(mesh):

time: 70 us -> 53 us (0.76)
  Pallas kernels: 61.7 us -> 48.9 us
  local copies, waits for them, and re-layouts: 6.73 us -> 0.68 us
  other arithmetic: 0 us -> 2 us
    pallas_call x1, Pallas kernels: 61.7 us -> 48.9 us  [body(): pl.pallas_call(functools.partial(kernel, groups=groups, tiles=tiles), out...]
    unnamed x6 -> x3, local copies, waits for them, and re-layouts: 6.73 us -> 0.68 us
    convert_element_type x0 -> x1, other arithmetic: none -> 2 us  [body(): return (feat.T.astype(F32), sums.T)]
where the time goes in v3:
time: 53 us; the launch traced here: 52.9 us
  Pallas kernels  48.9 us (92%)
  other arithmetic  2 us (4%)
  between operations  1.3 us (2%)
  local copies, waits for them, and re-layouts  0.68 us (1%)
    pallas_call x1, Pallas kernels, body(): pl.pallas_call(functools.partial(kernel, groups=groups, tiles=tiles), out...  48.9 us
    convert_element_type x1, other arithmetic, body(): return (feat.T.astype(F32), sums.T)  2 us

profile of v3, /device:TPU:1, one launch (start us, length us, event | category | flops | bytes accessed | tf_op | source)
XLA Modules:
  0.0 52.9 jit_solution(10045066661219150862)
XLA Ops:
  1.3 48.9 %shard_map.167 = (bf16[192,1024]{1,0:T(8,128)(2,1)}, f32[192,256]{1,0:T(8,128)}) custom-call(s32[1]{0:T(128)S(6)} %copy.19.count_ref, bf16[192,1024]{1,0:T(8,128)(2,1)} %bitcast.12, s32[8,128]{1,0:T(8,128)} %bitcast.15, f32[3,192]{1,0:T(4,128)} %pos_weight.1, f32[1,192]{1,0:T(1,128)} %bitcast.19, bf16[192,576]{1,0:T(8,128)(2,1)} %qkv_one.1, ...), custom_call_target="tpu_custom_call" | custom-call | tf_op jit(solution)/shard_map/pallas_call | solution.py:336
  50.2 0.0 copy-start
  50.2 2.0 %convert_bitcast_fusion = f32[1024,192]{0,1:T(8,128)} fusion(bf16[192,1024]{1,0:T(8,128)(2,1)} %get-tuple-element.4), kind=kLoop, calls=%fused_computation | loop fusion | flops 196608 | bytes 1179648 | tf_op jit(solution)/shard_map/convert_element_type | solution.py:375
  52.2 0.0 copy-done
  52.2 0.7 %copy.20 = f32[256,192]{0,1:T(8,128)} copy(f32[256,192]{0,1:T(8,128)S(1)} %bitcast.14) | data formatting | bytes 393216
Async XLA Ops:
  50.2 2.0 %copy-start = (f32[192,256]{1,0:T(8,128)S(1)}, f32[192,256]{1,0:T(8,128)}, u32[]{:S(2)}) copy-start(f32[192,256]{1,0:T(8,128)} %get-tuple-element.5) | copy-start | bytes 589828

commit v4 on v3

--- a/solution.py
+++ b/solution.py
@@ -17,6 +17,12 @@
 TN = (((0,), (0,)), ((), ()))
 MESH = pl.DeviceIdType.MESH
 LOG2E = 1.4426950408889634
+ENTER = 2
+VMEM_LIMIT = 24 * 2**20
+
+
+def spread_order(tiles):
+    return range(1, tiles)
 
 
 def iota(shape, dim):
@@ -149,67 +155,108 @@
     count_ref, nodes, ids, pos_weight, gain_one, qkv_one, out_one, gain_two, qkv_two, out_two,
     gain_three, w_up, w_down, slot_ref, owner_ref, voxel_ref,
     feat_out, vox_out,
-    start, in_one, proj_one, in_two, proj_two, up_turned, norm_one, norm_two, norm_three, sent_one, got_one, sent_two, got_two, count_sent, count_got,
-    vox_sent, vox_got, votes_sent, votes_got,
-    count_ss, count_rs, vox_ss, vox_rs, one_ss, one_rs, two_ss, two_rs, vote_ss, vote_rs,
+    start, in_one, proj_one, in_two, proj_two, up_turned, norm_one, norm_two, norm_three,
+    sent_one, got_one, sent_two, got_two, count_sent, count_got, vox_sent, vox_got, votes_sent, votes_got,
+    count_ss, count_rs, vox_ss, vox_rs, one_ss, one_rs, two_ss, two_rs, vote_ss, vote_rs, known,
     *, groups, tiles,
 ):
     me, tile = lax.axis_index("grp"), lax.axis_index("tile")
-    chans = nodes.shape[0]
+    chans, slots = nodes.shape
     chunks = start.shape[1]
     block = chunks * WIN
     run = WIN // groups
     rows = groups * WIN
     count = count_ref[0]
+    steps = [2**i for i in range(tiles.bit_length() - 1)]
+
+    def across(step):
+        return tile + step - 2 * step * lax.rem(tile // step, 2)
+
+    def grp_peer(d):
+        return lax.rem(me + d, groups)
+
+    def tile_peer(d):
+        return lax.rem(tile + d, tiles)
 
     barrier = pltpu.get_barrier_semaphore()
     for d in range(1, groups):
-        pl.semaphore_signal(barrier, inc=1, device_id=(lax.rem(me + d, groups), tile), device_id_type=MESH)
-    for d in range(1, tiles):
-        pl.semaphore_signal(barrier, inc=1, device_id=(me, lax.rem(tile + d, tiles)), device_id_type=MESH)
+        pl.semaphore_signal(barrier, inc=1, device_id=(grp_peer(d), tile), device_id_type=MESH)
+    for step in steps:
+        pl.semaphore_signal(barrier, inc=1, device_id=(me, across(step)), device_id_type=MESH)
+
+    def tell(i):
+        pl.semaphore_signal(known.at[i], inc=1, device_id=(me, across(steps[i])), device_id_type=MESH)
+
+    def told(i):
+        pl.semaphore_wait(known.at[i], 1)
 
     def to_group(d, src, dst, ss, rs):
-        return pltpu.make_async_remote_copy(
+        pltpu.make_async_remote_copy(
             src_ref=src, dst_ref=dst, send_sem=ss, recv_sem=rs,
-            device_id=(lax.rem(me + d, groups), tile), device_id_type=MESH,
-        )
+            device_id=(grp_peer(d), tile), device_id_type=MESH,
+        ).start()
 
     def to_tile(d, src, dst, ss, rs):
-        return pltpu.make_async_remote_copy(
+        pltpu.make_async_remote_copy(
             src_ref=src, dst_ref=dst, send_sem=ss, recv_sem=rs,
-            device_id=(me, lax.rem(tile + d, tiles)), device_id_type=MESH,
-        )
-
-    def count_copy(d):
-        return to_group(d, count_sent, count_got.at[me], count_ss.at[d], count_rs.at[d])
-
-    def vox_copy(d):
-        peer = lax.rem(tile + d, tiles)
-        return to_tile(d, vox_sent.at[peer], vox_got.at[tile], vox_ss.at[d], vox_rs.at[d])
-
-    def one_copy(d, c):
-        peer = lax.rem(me + d, groups)
-        return to_group(d, sent_one.at[c, peer], got_one.at[c, me], one_ss.at[c, d], one_rs.at[c, d])
-
-    def two_copy(d, c):
-        peer = lax.rem(me + d, groups)
-        return to_group(d, sent_two.at[c, peer], got_two.at[me, c], two_ss.at[c, d], two_rs.at[c, d])
-
-    def vote_copy(d):
-        peer = lax.rem(tile + d, tiles)
-        return to_tile(d, votes_sent.at[peer], votes_got.at[tile], vote_ss.at[d], vote_rs.at[d])
+            device_id=(me, tile_peer(d)), device_id_type=MESH,
+        ).start()
+
+    def settle(ref, sem):
+        pltpu.make_async_copy(ref, ref, sem).wait()
+
+    def send_one(c):
+        for d in range(1, groups):
+            to_group(d, sent_one.at[c, grp_peer(d)], got_one.at[c, me], one_ss, one_rs.at[c])
+
+    others = pl.ds(0, groups - 1)
+    rest = pl.ds(0, tiles - 1)
 
     count_sent[...] = jnp.full(count_sent.shape, count, jnp.int32)
     count_got[me] = jnp.full(count_sent.shape, count, jnp.int32)
     place_positions(start, nodes, ids[...], pos_weight[...])
     in_one[...] = turned(qkv_one[...])
+    proj_one[...] = turned(out_one[...])
+    norm_one[...] = jnp.broadcast_to(gain_one[...], (LANES, chans)).T
+
+    key = iota((WIN, LANES), 0)
+    window = iota((WIN, LANES), 1) // WIN
+
+    def stage_one(c, carry):
+        x = jnp.concatenate([start[g, c] for g in range(groups)], 0).astype(F32)
+        biases = []
+        for half in range(rows // LANES):
+            slot = (window + half * (LANES // WIN)) * block + c * WIN + key
+            kept = jnp.where(slot < count, 1.0, 0.0)
+            biases.append((kept - 1.0) * 1000000000.0)
+        first = attend(x.T, biases, norm_one[...], in_one[...], proj_one[...])
+        sent_one[c] = first.T.astype(BF16).reshape(groups, WIN, chans)
+        got_one[c, me] = sent_one[c, me]
+
+        @pl.when(c == ENTER)
+        def _():
+            pl.semaphore_wait(barrier, groups - 1 + len(steps))
+            for earlier in range(ENTER):
+                send_one(earlier)
+            for d in range(1, groups):
+                to_group(d, count_sent, count_got.at[me], count_ss, count_rs)
+            tell(1)
+
+        @pl.when(c >= ENTER)
+        def _():
+            send_one(c)
+
+        return carry
+
+    lax.fori_loop(0, chunks, stage_one, 0)
+    told(1)
+    tell(2)
+
     in_two[...] = turned(qkv_two[...])
-    proj_one[...] = turned(out_one[...])
     proj_two[...] = turned(out_two[...])
     up_turned[...] = turned(w_up[...])
-    for norm, gain in ((norm_one, gain_one), (norm_two, gain_two), (norm_three, gain_three)):
+    for norm, gain in ((norm_two, gain_two), (norm_three, gain_three)):
         norm[...] = jnp.broadcast_to(gain[...], (LANES, chans)).T
-
     votes = owner_ref.shape[1]
     owner = owner_ref[...].astype(F32)
     owner_col = columns(owner)
@@ -229,40 +276,16 @@
     for t in range(tiles):
         vox_sent[t] = jnp.broadcast_to(table[t : t + 1, :], vox_sent.shape[1:])
     vox_got[tile] = vox_sent[tile]
-
-    pl.semaphore_wait(barrier, groups + tiles - 2)
-    for d in range(1, groups):
-        count_copy(d).start()
-    for d in range(1, tiles):
-        vox_copy(d).start()
-
-    key = iota((WIN, LANES), 0)
-    window = iota((WIN, LANES), 1) // WIN
-
-    def stage_one(c, carry):
-        x = jnp.concatenate([start[g, c] for g in range(groups)], 0).astype(F32)
-        biases = []
-        for half in range(rows // LANES):
-            slot = (window + half * (LANES // WIN)) * block + c * WIN + key
-            kept = jnp.where(slot < count, 1.0, 0.0)
-            biases.append((kept - 1.0) * 1000000000.0)
-        first = attend(x.T, biases, norm_one[...], in_one[...], proj_one[...])
-        sent_one[c] = first.T.astype(BF16).reshape(groups, WIN, chans)
-        got_one[c, me] = sent_one[c, me]
-        for d in range(1, groups):
-            one_copy(d, c).start()
-        return carry
-
-    lax.fori_loop(0, chunks, stage_one, 0)
-
-    for d in range(1, groups):
-        count_copy(d).wait_recv()
+    told(2)
+    tell(3)
+
+    settle(count_got.at[others], count_rs)
     counts = jnp.zeros((WIN, LANES), jnp.int32)
     for g in range(groups):
         counts = jnp.where(key // run == g, count_got[g][:1, :], counts)
+
     def stage_two(c, carry):
-        for d in range(1, groups):
-            one_copy(d, c).wait_recv()
+        settle(got_one.at[c, others], one_rs.at[c])
         x = swapped(got_one[c].reshape(rows, chans).astype(F32), groups).T
         biases = []
         for half in range(rows // LANES):
@@ -274,18 +297,36 @@
         sent_two[c] = swapped(third.T, groups).astype(BF16).reshape(groups, WIN, chans)
         got_two[me, c] = sent_two[c, me]
         for d in range(1, groups):
-            two_copy(d, c).start()
+            to_group(d, sent_two.at[c, grp_peer(d)], got_two.at[me, c], two_ss, two_rs.at[c])
+
+        @pl.when(c == 0)
+        def _():
+            told(3)
+            tell(4)
+
+        @pl.when(c == 1)
+        def _():
+            told(4)
+            for d in range(1, tiles):
+                to_tile(d, vox_sent.at[tile_peer(d)], vox_got.at[tile], vox_ss, vox_rs)
+
         return carry
 
     lax.fori_loop(0, chunks, stage_two, 0)
 
-    slots = nodes.shape[1]
     slot_col = columns(slot_ref[...])
-    chosen = jnp.concatenate(
-        [(slot_col == (lane + LANES * t).astype(F32)).astype(BF16) for t in range(slots // LANES)], 1
-    )
-    for d in range(1, tiles):
-        vox_copy(d).wait_recv()
+
+    def pick(c):
+        chosen = []
+        for t in range(rows // LANES):
+            slot = (t * (LANES // WIN) + lane // WIN) * block + c * WIN + lane % WIN
+            chosen.append((slot_col == slot.astype(F32)).astype(BF16))
+        line = iota((rows, chans), 0)
+        kept = line // WIN * block + c * WIN + line % WIN < count
+        part = jnp.where(kept, got_two[:, c].reshape(rows, chans).astype(F32), 0.0).astype(BF16)
+        return mm(jnp.concatenate(chosen, 1), part)
+
+    settle(vox_got.at[rest], vox_rs)
     vox = iota((VOX_DEV, LANES), 0).astype(F32)
     sums = []
     for a in range(tiles // share):
@@ -294,31 +335,44 @@
             mine = mine + vox_got[share * a + u]
         sums.append((vox == mine[:1, :]).astype(BF16))
     sums = jnp.concatenate(sums, 1)
-
+    packing = (iota((tiles * CAP, votes), 0).astype(F32) == place).astype(BF16)
+    picked = None
     for c in range(chunks):
-        for d in range(1, groups):
-            two_copy(d, c).wait_recv()
+        settle(got_two.at[others, c], two_rs.at[c])
+        part = pick(c)
+        picked = part if picked is None else picked + part
+    picked = picked.astype(BF16)
+
+    per = tiles // 4
+    short = chans - LANES
+    for q in range(4):
+        mine = mm(packing[q * per * CAP : (q + 1) * per * CAP], picked).reshape(per, CAP, chans)
+        tail = mine[:, :, LANES:]
+        tail = jnp.concatenate([tail[:, : CAP // 2], tail[:, CAP // 2 :]], 2)
+        votes_sent[q * per : (q + 1) * per] = jnp.concatenate([mine[:, :, :LANES], tail], 1).astype(BF16)
+    votes_got[tile] = votes_sent[tile]
+    for d in spread_order(tiles):
+        to_tile(d, votes_sent.at[tile_peer(d)], votes_got.at[tile], vote_ss, vote_rs)
+
     back = got_two[...].reshape(slots, chans)
-    feat = jnp.where(iota((slots, chans), 0) < count, back.astype(F32), 0.0).astype(BF16)
-    feat_out[...] = feat.astype(F32).T.astype(BF16)
-    picked = mm(chosen, feat).astype(BF16)
-    packing = (iota((tiles * CAP, votes), 0).astype(F32) == place).astype(BF16)
-    votes_sent[...] = mm(packing, picked).astype(BF16).reshape(tiles, CAP, chans)
-    votes_got[tile] = votes_sent[tile]
-    for d in range(1, tiles):
-        vote_copy(d).start()
-    for d in range(1, tiles):
-        vote_copy(d).wait_recv()
-    vox_out[...] = mm(sums, votes_got[...].reshape(tiles * CAP, chans)).T
-
-    for d in range(1, groups):
-        count_copy(d).wait_send()
-        for c in range(chunks):
-            one_copy(d, c).wait_send()
-            two_copy(d, c).wait_send()
-    for d in range(1, tiles):
-        vox_copy(d).wait_send()
-        vote_copy(d).wait_send()
+    feat = jnp.where(iota((slots, chans), 0) < count, back.astype(F32), 0.0)
+    feat_out[...] = feat.T.astype(BF16)
+    settle(count_got.at[others], count_ss)
+    settle(got_one.at[:, others], one_ss)
+    settle(got_two.at[others, :], two_ss)
+    settle(vox_got.at[rest], vox_ss)
+    settle(votes_got.at[rest], vote_ss)
+
+    settle(votes_got.at[rest], vote_rs)
+    head = votes_got[:, :CAP, :].reshape(tiles * CAP, LANES)
+    tail = votes_got[:, CAP:, :].astype(F32)
+    tail = jnp.concatenate([tail[:, :, :short], tail[:, :, short:]], 1).reshape(tiles * CAP, short).astype(BF16)
+    vox_out[...] = mm(sums, jnp.concatenate([head, tail], 1)).T
+
+
+def finish(feat, sums, feat_out, sums_out):
+    feat_out[...] = feat[...].astype(F32)
+    sums_out[...] = sums[...]
 
 
 def body(
@@ -359,20 +413,29 @@
             pltpu.VMEM((groups, 8, LANES), jnp.int32),
             pltpu.VMEM((tiles, 8, LANES), F32),
             pltpu.VMEM((tiles, 8, LANES), F32),
-            pltpu.VMEM((tiles, CAP, chans), BF16),
-            pltpu.VMEM((tiles, CAP, chans), BF16),
-            dma((groups,)), dma((groups,)), dma((tiles,)), dma((tiles,)),
-            dma((chunks, groups)), dma((chunks, groups)), dma((chunks, groups)), dma((chunks, groups)),
-            dma((tiles,)), dma((tiles,)),
+            pltpu.VMEM((tiles, CAP * 3 // 2, LANES), BF16),
+            pltpu.VMEM((tiles, CAP * 3 // 2, LANES), BF16),
+            dma, dma, dma, dma, dma, dma((chunks,)), dma, dma((chunks,)), dma, dma,
+            pltpu.SemaphoreType.REGULAR((tiles.bit_length() - 1,)),
         ],
-        compiler_params=pltpu.CompilerParams(collective_id=0, has_side_effects=True),
+        compiler_params=pltpu.CompilerParams(collective_id=0, has_side_effects=True, vmem_limit_bytes=VMEM_LIMIT),
     )(
         node_count, nodes.T, node_ids.reshape(slots // LANES, LANES), pos_weight,
         gain_one.reshape(1, chans), qkv_one, out_one, gain_two.reshape(1, chans), qkv_two, out_two,
         gain_three.reshape(1, chans), w_up, w_down.T,
         vote_slot.reshape(1, votes), vote_owner.reshape(1, votes), vote_voxel.reshape(1, votes),
     )
-    return feat.T.astype(F32), sums.T
+    feat, sums = pl.pallas_call(
+        finish,
+        out_shape=(
+            jax.ShapeDtypeStruct((chans, slots), F32),
+            jax.ShapeDtypeStruct((chans, VOX_DEV), F32),
+        ),
+        in_specs=[vmem, vmem],
+        out_specs=(vmem, vmem),
+        compiler_params=pltpu.CompilerParams(vmem_limit_bytes=8 * 2**20),
+    )(feat, sums)
+    return feat.T, sums.T
 
 
 def solution(mesh):

time: 53 us -> 52.6 us (level)
  local copies, waits for them, and re-layouts: 0.68 us -> 7.31 us
  Pallas kernels: 48.9 us -> 43.6 us
  other arithmetic: 2 us -> 0 us
    unnamed x3 -> x30, local copies, waits for them, and re-layouts: 0.68 us -> 7.31 us
    pallas_call x1, Pallas kernels: 48.9 us -> 42.6 us  [body(): pl.pallas_call(functools.partial(kernel, groups=groups, tiles=tiles), out...]
    convert_element_type x1 -> x0, other arithmetic: 2 us -> none  [body(): return (feat.T.astype(F32), sums.T)]
    pallas_call x0 -> x1, Pallas kernels: none -> 1.01 us  [body(): pl.pallas_call(finish, out_shape=(jax.ShapeDtypeStruct((chans, slots), F3...]
where the time goes in v4:
time: 52.6 us; the launch traced here: 52.2 us
  Pallas kernels  43.6 us (83%)
  local copies, waits for them, and re-layouts  7.31 us (14%)
  between operations  1.36 us (3%)
    pallas_call x1, Pallas kernels, body(): pl.pallas_call(functools.partial(kernel, groups=groups, tiles=tiles), out...  42.6 us
    unnamed x30, local copies, waits for them, and re-layouts  7.31 us

profile of v4, /device:TPU:1, one launch (start us, length us, event | category | flops | bytes accessed | tf_op | source)
XLA Modules:
  0.0 52.2 jit_solution(6567981857437066131)
XLA Ops:
  1.3 0.0 copy-start.13
  1.3 0.0 copy-start.14
  1.3 0.0 copy-start.11
  1.3 0.0 copy-start.10
  1.3 0.0 copy-start.9
  1.3 0.0 copy-start.8
  1.3 0.0 copy-start.7
  1.4 0.0 copy-start.12
  1.4 0.6 %copy-done.13 = f32[192]{0:T(256)S(1)} copy-done((f32[192]{0:T(256)S(1)}, f32[192]{0:T(256)}, u32[]{:S(2)}) %copy-start.13) | copy-done | bytes 792
  2.0 0.0 copy-done.14
  2.0 0.0 copy-done.11
  2.0 0.0 copy-done.10
  2.0 0.0 copy-done.9
  2.0 0.0 copy-done.8
  2.0 0.0 copy-done.7
  2.1 0.0 copy-done.12
  2.1 0.0 copy-start
  2.1 1.0 %copy-done = bf16[1024,192]{0,1:T(8,128)(2,1)S(1)} copy-done((bf16[1024,192]{0,1:T(8,128)(2,1)S(1)}, bf16[1024,192]{0,1:T(8,128)(2,1)}, u32[]{:S(2)}) %copy-start) | copy-done | bytes 393240
  3.1 0.0 copy-start.1
  3.1 1.0 %copy-done.1 = bf16[192,768]{1,0:T(8,128)(2,1)S(1)} copy-done((bf16[192,768]{1,0:T(8,128)(2,1)S(1)}, bf16[192,768]{1,0:T(8,128)(2,1)}, u32[]{:S(2)}) %copy-start.1) | copy-done | bytes 294936
  4.0 0.0 copy-start.2
  4.0 1.0 %copy-done.2 = bf16[768,192]{0,1:T(8,128)(2,1)S(1)} copy-done((bf16[768,192]{0,1:T(8,128)(2,1)S(1)}, bf16[768,192]{0,1:T(8,128)(2,1)}, u32[]{:S(2)}) %copy-start.2) | copy-done | bytes 294936
  5.0 0.0 copy-start.3
  5.0 0.9 %copy-done.3 = bf16[192,576]{1,0:T(8,128)(2,1)S(1)} copy-done((bf16[192,576]{1,0:T(8,128)(2,1)S(1)}, bf16[192,576]{1,0:T(8,128)(2,1)}, u32[]{:S(2)}) %copy-start.3) | copy-done | bytes 221208
  5.9 0.0 copy-start.4
  5.9 0.9 %copy-done.4 = bf16[192,576]{1,0:T(8,128)(2,1)S(1)} copy-done((bf16[192,576]{1,0:T(8,128)(2,1)S(1)}, bf16[192,576]{1,0:T(8,128)(2,1)}, u32[]{:S(2)}) %copy-start.4) | copy-done | bytes 221208
  6.9 0.0 copy-start.5
  6.9 0.9 %copy-done.5 = bf16[192,192]{1,0:T(8,128)(2,1)S(1)} copy-done((bf16[192,192]{1,0:T(8,128)(2,1)S(1)}, bf16[192,192]{1,0:T(8,128)(2,1)}, u32[]{:S(2)}) %copy-start.5) | copy-done | bytes 73752
  7.8 0.0 copy-start.6
  7.8 0.9 %copy-done.6 = bf16[192,192]{1,0:T(8,128)(2,1)S(1)} copy-done((bf16[192,192]{1,0:T(8,128)(2,1)S(1)}, bf16[192,192]{1,0:T(8,128)(2,1)}, u32[]{:S(2)}) %copy-start.6) | copy-done | bytes 73752
  8.7 42.6 %shard_map.167 = (bf16[192,1024]{1,0:T(8,128)(2,1)S(1)}, f32[192,256]{1,0:T(8,128)S(1)}) custom-call(s32[1]{0:T(128)S(6)} %copy.18.count_ref, bf16[192,1024]{1,0:T(8,128)(2,1)S(1)} %bitcast.11, s32[8,128]{1,0:T(8,128)S(1)} %bitcast.13, f32[3,192]{1,0:T(4,128)S(1)} %copy-done.8, f32[1,192]{1,0:T(1,128)S(1)} %bitcast.17, bf16[192,576]{1,0:T(8,128)(2,1)S(1)} %copy-done.3, ...), custom_call_target="tpu_custom_call" | custom-call | tf_op jit(solution)/shard_map/pallas_call | solution.py:390
  51.2 1.0 %shard_map.168 = (f32[192,1024]{1,0:T(8,128)}, f32[192,256]{1,0:T(8,128)}) custom-call(bf16[192,1024]{1,0:T(8,128)(2,1)S(1)} %get-tuple-element.6.feat, f32[192,256]{1,0:T(8,128)S(1)} %get-tuple-element.7.sums), custom_call_target="tpu_custom_call" | custom-call | tf_op jit(solution)/shard_map/pallas_call | solution.py:428
Async XLA Ops:
  1.3 0.7 %copy-start.13 = (f32[192]{0:T(256)S(1)}, f32[192]{0:T(256)}, u32[]{:S(2)}) copy-start(f32[192]{0:T(256)} %param.23) | copy-start | bytes 2308
  1.3 0.7 %copy-start.14 = (f32[192]{0:T(256)S(1)}, f32[192]{0:T(256)}, u32[]{:S(2)}) copy-start(f32[192]{0:T(256)} %param.26) | copy-start | bytes 2308
  1.3 0.7 %copy-start.11 = (s32[512]{0:T(512)S(1)}, s32[512]{0:T(512)}, u32[]{:S(2)}) copy-start(s32[512]{0:T(512)} %param.31) | copy-start | bytes 6148
  1.3 0.7 %copy-start.10 = (s32[512,1]{0,1:T(1,128)S(1)}, s32[512,1]{0,1:T(1,128)}, u32[]{:S(2)}) copy-start(s32[512,1]{0,1:T(1,128)} %param.30) | copy-start | bytes 6148
  1.3 0.7 %copy-start.9 = (s32[512]{0:T(512)S(1)}, s32[512]{0:T(512)}, u32[]{:S(2)}) copy-start(s32[512]{0:T(512)} %param.29) | copy-start | bytes 6148
  1.3 0.7 %copy-start.8 = (f32[3,192]{1,0:T(4,128)S(1)}, f32[3,192]{1,0:T(4,128)}, u32[]{:S(2)}) copy-start(f32[3,192]{1,0:T(4,128)} %pos_weight.1) | copy-start | bytes 6916
  1.3 0.7 %copy-start.7 = (s32[1024]{0:T(1024)S(1)}, s32[1024]{0:T(1024)}, u32[]{:S(2)}) copy-start(s32[1024]{0:T(1024)} %param.17) | copy-start | bytes 12292
  1.4 0.7 %copy-start.12 = (f32[192]{0:T(256)S(1)}, f32[192]{0:T(256)}, u32[]{:S(2)}) copy-start(f32[192]{0:T(256)} %param.20) | copy-start | bytes 2308
  2.1 1.0 %copy-start = (bf16[1024,192]{0,1:T(8,128)(2,1)S(1)}, bf16[1024,192]{0,1:T(8,128)(2,1)}, u32[]{:S(2)}) copy-start(bf16[1024,192]{0,1:T(8,128)(2,1)} %param.16) | copy-start | bytes 1179652
  3.1 1.0 %copy-start.1 = (bf16[192,768]{1,0:T(8,128)(2,1)S(1)}, bf16[192,768]{1,0:T(8,128)(2,1)}, u32[]{:S(2)}) copy-start(bf16[192,768]{1,0:T(8,128)(2,1)} %w_up.1) | copy-start | bytes 884740
  4.0 1.0 %copy-start.2 = (bf16[768,192]{0,1:T(8,128)(2,1)S(1)}, bf16[768,192]{0,1:T(8,128)(2,1)}, u32[]{:S(2)}) copy-start(bf16[768,192]{0,1:T(8,128)(2,1)} %param.28) | copy-start | bytes 884740
  5.0 0.9 %copy-start.3 = (bf16[192,576]{1,0:T(8,128)(2,1)S(1)}, bf16[192,576]{1,0:T(8,128)(2,1)}, u32[]{:S(2)}) copy-start(bf16[192,576]{1,0:T(8,128)(2,1)} %qkv_one.1) | copy-start | bytes 663556
  5.9 0.9 %copy-start.4 = (bf16[192,576]{1,0:T(8,128)(2,1)S(1)}, bf16[192,576]{1,0:T(8,128)(2,1)}, u32[]{:S(2)}) copy-start(bf16[192,576]{1,0:T(8,128)(2,1)} %qkv_two.1) | copy-start | bytes 663556
  6.9 0.9 %copy-start.5 = (bf16[192,192]{1,0:T(8,128)(2,1)S(1)}, bf16[192,192]{1,0:T(8,128)(2,1)}, u32[]{:S(2)}) copy-start(bf16[192,192]{1,0:T(8,128)(2,1)} %out_one.1) | copy-start | bytes 221188
  7.8 0.9 %copy-start.6 = (bf16[192,192]{1,0:T(8,128)(2,1)S(1)}, bf16[192,192]{1,0:T(8,128)(2,1)}, u32[]{:S(2)}) copy-start(bf16[192,192]{1,0:T(8,128)(2,1)} %out_two.1) | copy-start | bytes 221188

commit v5 on v4

--- a/solution.py
+++ b/solution.py
@@ -18,11 +18,16 @@
 MESH = pl.DeviceIdType.MESH
 LOG2E = 1.4426950408889634
 ENTER = 2
-VMEM_LIMIT = 24 * 2**20
-
-
-def spread_order(tiles):
-    return range(1, tiles)
+INPUTS = 15
+FIRST = (0, 1, 2, 4, 5, 3)
+LATER = (7, 8, 6, 9, 10, 11, 13, 14, 12)
+
+
+ROWS = 4
+
+
+def by_distance(n):
+    return sorted(range(n), key=lambda d: (-min(d, n - d), d))
 
 
 def iota(shape, dim):
@@ -152,14 +157,19 @@
 
 
 def kernel(
-    count_ref, nodes, ids, pos_weight, gain_one, qkv_one, out_one, gain_two, qkv_two, out_two,
-    gain_three, w_up, w_down, slot_ref, owner_ref, voxel_ref,
-    feat_out, vox_out,
+    count_ref, *refs, groups, tiles,
+):
+    far, (feat_out, vox_out), near = refs[:INPUTS], refs[INPUTS : INPUTS + 2], refs[INPUTS + 2 : 2 * INPUTS + 2]
+    (
+        nodes, ids, pos_weight, gain_one, qkv_one, out_one, gain_two, qkv_two, out_two,
+        gain_three, w_up, w_down, slot_ref, owner_ref, voxel_ref,
+    ) = near
+    loads = refs[2 * INPUTS + 2]
+    (
     start, in_one, proj_one, in_two, proj_two, up_turned, norm_one, norm_two, norm_three,
     sent_one, got_one, sent_two, got_two, count_sent, count_got, vox_sent, vox_got, votes_sent, votes_got,
-    count_ss, count_rs, vox_ss, vox_rs, one_ss, one_rs, two_ss, two_rs, vote_ss, vote_rs, known,
-    *, groups, tiles,
-):
+    count_ss, count_rs, vox_ss, vox_rs, one_ss, one_rs, two_ss, two_rs, vote_ss, vote_rs, known, turned_feat, feat_sem,
+    ) = refs[2 * INPUTS + 3 :]
     me, tile = lax.axis_index("grp"), lax.axis_index("tile")
     chans, slots = nodes.shape
     chunks = start.shape[1]
@@ -184,6 +194,13 @@
     for step in steps:
         pl.semaphore_signal(barrier, inc=1, device_id=(me, across(step)), device_id_type=MESH)
 
+    for i in FIRST + LATER:
+        pltpu.make_async_copy(far[i], near[i], loads.at[i]).start()
+
+    def loaded(which):
+        for i in which:
+            pltpu.make_async_copy(far[i], near[i], loads.at[i]).wait()
+
     def tell(i):
         pl.semaphore_signal(known.at[i], inc=1, device_id=(me, across(steps[i])), device_id_type=MESH)
 
@@ -196,10 +213,10 @@
             device_id=(grp_peer(d), tile), device_id_type=MESH,
         ).start()
 
-    def to_tile(d, src, dst, ss, rs):
+    def to_tile(peer, src, dst, ss, rs):
         pltpu.make_async_remote_copy(
             src_ref=src, dst_ref=dst, send_sem=ss, recv_sem=rs,
-            device_id=(me, tile_peer(d)), device_id_type=MESH,
+            device_id=(me, peer), device_id_type=MESH,
         ).start()
 
     def settle(ref, sem):
@@ -212,6 +229,7 @@
     others = pl.ds(0, groups - 1)
     rest = pl.ds(0, tiles - 1)
 
+    loaded(FIRST)
     count_sent[...] = jnp.full(count_sent.shape, count, jnp.int32)
     count_got[me] = jnp.full(count_sent.shape, count, jnp.int32)
     place_positions(start, nodes, ids[...], pos_weight[...])
@@ -252,6 +270,7 @@
     told(1)
     tell(2)
 
+    loaded(LATER)
     in_two[...] = turned(qkv_two[...])
     proj_two[...] = turned(out_two[...])
     up_turned[...] = turned(w_up[...])
@@ -308,7 +327,7 @@
         def _():
             told(4)
             for d in range(1, tiles):
-                to_tile(d, vox_sent.at[tile_peer(d)], vox_got.at[tile], vox_ss, vox_rs)
+                to_tile(tile_peer(d), vox_sent.at[tile_peer(d)], vox_got.at[tile], vox_ss, vox_rs)
 
         return carry
 
@@ -335,7 +354,6 @@
             mine = mine + vox_got[share * a + u]
         sums.append((vox == mine[:1, :]).astype(BF16))
     sums = jnp.concatenate(sums, 1)
-    packing = (iota((tiles * CAP, votes), 0).astype(F32) == place).astype(BF16)
     picked = None
     for c in range(chunks):
         settle(got_two.at[others, c], two_rs.at[c])
@@ -343,25 +361,34 @@
         picked = part if picked is None else picked + part
     picked = picked.astype(BF16)
 
-    per = tiles // 4
-    short = chans - LANES
-    for q in range(4):
-        mine = mm(packing[q * per * CAP : (q + 1) * per * CAP], picked).reshape(per, CAP, chans)
+    deep = tiles // ROWS
+    here, along = tile // deep, lax.rem(tile, deep)
+    line = iota((deep * CAP, votes), 0)
+    for y in by_distance(ROWS):
+        row = lax.rem(here + y, ROWS)
+        packing = ((line + row * deep * CAP).astype(F32) == place).astype(BF16)
+        mine = mm(packing, picked).reshape(deep, CAP, chans)
         tail = mine[:, :, LANES:]
         tail = jnp.concatenate([tail[:, : CAP // 2], tail[:, CAP // 2 :]], 2)
-        votes_sent[q * per : (q + 1) * per] = jnp.concatenate([mine[:, :, :LANES], tail], 1).astype(BF16)
+        votes_sent[pl.ds(row * deep, deep)] = jnp.concatenate([mine[:, :, :LANES], tail], 1).astype(BF16)
+        for z in by_distance(deep):
+            if y or z:
+                peer = row * deep + lax.rem(along + z, deep)
+                to_tile(peer, votes_sent.at[peer], votes_got.at[tile], vote_ss, vote_rs)
     votes_got[tile] = votes_sent[tile]
-    for d in spread_order(tiles):
-        to_tile(d, votes_sent.at[tile_peer(d)], votes_got.at[tile], vote_ss, vote_rs)
-
+
+    short = chans - LANES
     back = got_two[...].reshape(slots, chans)
     feat = jnp.where(iota((slots, chans), 0) < count, back.astype(F32), 0.0)
-    feat_out[...] = feat.T.astype(BF16)
+    turned_feat[...] = feat.T.astype(BF16)
+    leave = pltpu.make_async_copy(turned_feat, feat_out, feat_sem)
+    leave.start()
     settle(count_got.at[others], count_ss)
     settle(got_one.at[:, others], one_ss)
     settle(got_two.at[others, :], two_ss)
     settle(vox_got.at[rest], vox_ss)
     settle(votes_got.at[rest], vote_ss)
+    leave.wait()
 
     settle(votes_got.at[rest], vote_rs)
     head = votes_got[:, :CAP, :].reshape(tiles * CAP, LANES)
@@ -384,6 +411,12 @@
     groups, tiles = lax.axis_size("grp"), lax.axis_size("tile")
     chunks = slots // groups // WIN
     vmem = pl.BlockSpec(memory_space=pltpu.VMEM)
+    inputs = (
+        nodes.T, node_ids.reshape(slots // LANES, LANES), pos_weight,
+        gain_one.reshape(1, chans), qkv_one, out_one, gain_two.reshape(1, chans), qkv_two, out_two,
+        gain_three.reshape(1, chans), w_up, w_down.T,
+        vote_slot.reshape(1, votes), vote_owner.reshape(1, votes), vote_voxel.reshape(1, votes),
+    )
     dma = pltpu.SemaphoreType.DMA
 
 
@@ -393,9 +426,11 @@
             jax.ShapeDtypeStruct((chans, slots), BF16),
             jax.ShapeDtypeStruct((chans, VOX_DEV), F32),
         ),
-        in_specs=[pl.BlockSpec(memory_space=pltpu.SMEM)] + [vmem] * 15,
-        out_specs=(vmem, vmem),
-        scratch_shapes=[
+        in_specs=[pl.BlockSpec(memory_space=pltpu.SMEM)] + [pl.BlockSpec(memory_space=pltpu.HBM)] * INPUTS,
+        out_specs=(pl.BlockSpec(memory_space=pltpu.HBM), vmem),
+        scratch_shapes=[pltpu.VMEM(i.shape, i.dtype) for i in inputs]
+        + [
+            dma((INPUTS,)),
             pltpu.VMEM((groups, chunks, WIN, chans), BF16),
             pltpu.VMEM((3 * chans, chans), BF16),
             pltpu.VMEM((chans, chans), BF16),
@@ -417,13 +452,12 @@
             pltpu.VMEM((tiles, CAP * 3 // 2, LANES), BF16),
             dma, dma, dma, dma, dma, dma((chunks,)), dma, dma((chunks,)), dma, dma,
             pltpu.SemaphoreType.REGULAR((tiles.bit_length() - 1,)),
+            pltpu.VMEM((chans, slots), BF16),
+            dma,
         ],
-        compiler_params=pltpu.CompilerParams(collective_id=0, has_side_effects=True, vmem_limit_bytes=VMEM_LIMIT),
+        compiler_params=pltpu.CompilerParams(collective_id=0, has_side_effects=True),
     )(
-        node_count, nodes.T, node_ids.reshape(slots // LANES, LANES), pos_weight,
-        gain_one.reshape(1, chans), qkv_one, out_one, gain_two.reshape(1, chans), qkv_two, out_two,
-        gain_three.reshape(1, chans), w_up, w_down.T,
-        vote_slot.reshape(1, votes), vote_owner.reshape(1, votes), vote_voxel.reshape(1, votes),
+        node_count, *inputs
     )
     feat, sums = pl.pallas_call(
         finish,
@@ -433,7 +467,6 @@
         ),
         in_specs=[vmem, vmem],
         out_specs=(vmem, vmem),
-        compiler_params=pltpu.CompilerParams(vmem_limit_bytes=8 * 2**20),
     )(feat, sums)
     return feat.T, sums.T
 

time: 52.6 us -> 47.3 us (0.90)
  local copies, waits for them, and re-layouts: 7.31 us -> 0 us
  Pallas kernels: 43.6 us -> 45.8 us
    unnamed x30 -> x0, local copies, waits for them, and re-layouts: 7.31 us -> none
    pallas_call x1, Pallas kernels: 42.6 us -> 43.8 us  [body(): pl.pallas_call(functools.partial(kernel, groups=groups, tiles=tiles), out...]
    pallas_call x1, Pallas kernels: 1.01 us -> 2.05 us  [body(): pl.pallas_call(finish, out_shape=(jax.ShapeDtypeStruct((chans, slots), F3...]
where the time goes in v5:
time: 47.3 us; the launch traced here: 47.1 us
  Pallas kernels  45.8 us (97%)
  between operations  1.29 us (3%)
    pallas_call x1, Pallas kernels, body(): pl.pallas_call(functools.partial(kernel, groups=groups, tiles=tiles), out...  43.8 us
    pallas_call x1, Pallas kernels, body(): pl.pallas_call(finish, out_shape=(jax.ShapeDtypeStruct((chans, slots), F3...  2.05 us

profile of v5, /device:TPU:1, one launch (start us, length us, event | category | flops | bytes accessed | tf_op | source)
XLA Modules:
  0.0 47.1 jit_solution(16733085469596274017)
XLA Ops:
  1.3 43.8 %shard_map.167 = (bf16[192,1024]{1,0:T(8,128)(2,1)}, f32[192,256]{1,0:T(8,128)}) custom-call(s32[1]{0:T(128)S(6)} %copy.18.count_ref, bf16[192,1024]{1,0:T(8,128)(2,1)} %bitcast.11, s32[8,128]{1,0:T(8,128)} %bitcast.13, f32[3,192]{1,0:T(4,128)} %refs_2_.1, f32[1,192]{1,0:T(1,128)} %bitcast.17, bf16[192,576]{1,0:T(8,128)(2,1)} %refs_4_.1, ...), custom_call_target="tpu_custom_call" | custom-call | tf_op jit(solution)/shard_map/pallas_call | solution.py:423
  45.1 2.1 %shard_map.168 = (f32[192,1024]{1,0:T(8,128)}, f32[192,256]{1,0:T(8,128)}) custom-call(bf16[192,1024]{1,0:T(8,128)(2,1)} %get-tuple-element.6.feat, f32[192,256]{1,0:T(8,128)} %get-tuple-element.7.sums), custom_call_target="tpu_custom_call" | custom-call | tf_op jit(solution)/shard_map/pallas_call | solution.py:462

commit v6 on v5

--- a/solution.py
+++ b/solution.py
@@ -17,13 +17,15 @@
 TN = (((0,), (0,)), ((), ()))
 MESH = pl.DeviceIdType.MESH
 LOG2E = 1.4426950408889634
-ENTER = 2
 INPUTS = 15
 FIRST = (0, 1, 2, 4, 5, 3)
 LATER = (7, 8, 6, 9, 10, 11, 13, 14, 12)
 
 
 ROWS = 4
+PIECE = 48
+UNROLL = 2
+UNROLL_TWO = 1
 
 
 def by_distance(n):
@@ -168,7 +170,7 @@
     (
     start, in_one, proj_one, in_two, proj_two, up_turned, norm_one, norm_two, norm_three,
     sent_one, got_one, sent_two, got_two, count_sent, count_got, vox_sent, vox_got, votes_sent, votes_got,
-    count_ss, count_rs, vox_ss, vox_rs, one_ss, one_rs, two_ss, two_rs, vote_ss, vote_rs, known, turned_feat, feat_sem,
+    count_ss, count_rs, vox_ss, vox_rs, one_ss, one_rs, two_ss, two_rs, vote_ss, vote_rs, known, turned_feat, feat_sem, sums_of,
     ) = refs[2 * INPUTS + 3 :]
     me, tile = lax.axis_index("grp"), lax.axis_index("tile")
     chans, slots = nodes.shape
@@ -240,33 +242,31 @@
     key = iota((WIN, LANES), 0)
     window = iota((WIN, LANES), 1) // WIN
 
-    def stage_one(c, carry):
-        x = jnp.concatenate([start[g, c] for g in range(groups)], 0).astype(F32)
-        biases = []
-        for half in range(rows // LANES):
-            slot = (window + half * (LANES // WIN)) * block + c * WIN + key
-            kept = jnp.where(slot < count, 1.0, 0.0)
-            biases.append((kept - 1.0) * 1000000000.0)
-        first = attend(x.T, biases, norm_one[...], in_one[...], proj_one[...])
-        sent_one[c] = first.T.astype(BF16).reshape(groups, WIN, chans)
-        got_one[c, me] = sent_one[c, me]
-
-        @pl.when(c == ENTER)
+    def stage_one(step, carry):
+        here = [step * UNROLL + u for u in range(UNROLL)]
+        for c in here:
+            x = jnp.concatenate([start[g, c] for g in range(groups)], 0).astype(F32)
+            biases = []
+            for half in range(rows // LANES):
+                slot = (window + half * (LANES // WIN)) * block + c * WIN + key
+                kept = jnp.where(slot < count, 1.0, 0.0)
+                biases.append((kept - 1.0) * 1000000000.0)
+            first = attend(x.T, biases, norm_one[...], in_one[...], proj_one[...])
+            sent_one[c] = first.T.astype(BF16).reshape(groups, WIN, chans)
+
+        @pl.when(step == 0)
         def _():
             pl.semaphore_wait(barrier, groups - 1 + len(steps))
-            for earlier in range(ENTER):
-                send_one(earlier)
             for d in range(1, groups):
                 to_group(d, count_sent, count_got.at[me], count_ss, count_rs)
             tell(1)
 
-        @pl.when(c >= ENTER)
-        def _():
+        for c in here:
+            got_one[c, me] = sent_one[c, me]
             send_one(c)
-
         return carry
 
-    lax.fori_loop(0, chunks, stage_one, 0)
+    lax.fori_loop(0, chunks // UNROLL, stage_one, 0)
     told(1)
     tell(2)
 
@@ -303,27 +303,31 @@
     for g in range(groups):
         counts = jnp.where(key // run == g, count_got[g][:1, :], counts)
 
-    def stage_two(c, carry):
-        settle(got_one.at[c, others], one_rs.at[c])
-        x = swapped(got_one[c].reshape(rows, chans).astype(F32), groups).T
-        biases = []
-        for half in range(rows // LANES):
-            slot = me * block + c * WIN + (half * (LANES // WIN) + window) * run + key % run
-            kept = jnp.where(slot < counts, 1.0, 0.0)
-            biases.append((kept - 1.0) * 1000000000.0)
-        second = attend(x, biases, norm_two[...], in_two[...], proj_two[...])
-        third = feed(second, norm_three[...], up_turned[...], w_down[...])
-        sent_two[c] = swapped(third.T, groups).astype(BF16).reshape(groups, WIN, chans)
-        got_two[me, c] = sent_two[c, me]
-        for d in range(1, groups):
-            to_group(d, sent_two.at[c, grp_peer(d)], got_two.at[me, c], two_ss, two_rs.at[c])
-
-        @pl.when(c == 0)
+    def stage_two(step, carry):
+        here = [step * UNROLL_TWO + u for u in range(UNROLL_TWO)]
+        for c in here:
+            settle(got_one.at[c, others], one_rs.at[c])
+        for c in here:
+            x = swapped(got_one[c].reshape(rows, chans).astype(F32), groups).T
+            biases = []
+            for half in range(rows // LANES):
+                slot = me * block + c * WIN + (half * (LANES // WIN) + window) * run + key % run
+                kept = jnp.where(slot < counts, 1.0, 0.0)
+                biases.append((kept - 1.0) * 1000000000.0)
+            second = attend(x, biases, norm_two[...], in_two[...], proj_two[...])
+            third = feed(second, norm_three[...], up_turned[...], w_down[...])
+            sent_two[c] = swapped(third.T, groups).astype(BF16).reshape(groups, WIN, chans)
+        for c in here:
+            got_two[me, c] = sent_two[c, me]
+            for d in range(1, groups):
+                to_group(d, sent_two.at[c, grp_peer(d)], got_two.at[me, c], two_ss, two_rs.at[c])
+
+        @pl.when(step == 0)
         def _():
             told(3)
             tell(4)
 
-        @pl.when(c == 1)
+        @pl.when(step == 1)
         def _():
             told(4)
             for d in range(1, tiles):
@@ -331,7 +335,7 @@
 
         return carry
 
-    lax.fori_loop(0, chunks, stage_two, 0)
+    lax.fori_loop(0, chunks // UNROLL_TWO, stage_two, 0)
 
     slot_col = columns(slot_ref[...])
 
@@ -353,7 +357,10 @@
         for u in range(1, share):
             mine = mine + vox_got[share * a + u]
         sums.append((vox == mine[:1, :]).astype(BF16))
-    sums = jnp.concatenate(sums, 1)
+    deep = tiles // ROWS
+    wide = deep // share
+    for q in range(ROWS):
+        sums_of[q] = jnp.concatenate(sums[q * wide : (q + 1) * wide], 1)
     picked = None
     for c in range(chunks):
         settle(got_two.at[others, c], two_rs.at[c])
@@ -361,7 +368,6 @@
         picked = part if picked is None else picked + part
     picked = picked.astype(BF16)
 
-    deep = tiles // ROWS
     here, along = tile // deep, lax.rem(tile, deep)
     line = iota((deep * CAP, votes), 0)
     for y in by_distance(ROWS):
@@ -374,7 +380,7 @@
         for z in by_distance(deep):
             if y or z:
                 peer = row * deep + lax.rem(along + z, deep)
-                to_tile(peer, votes_sent.at[peer], votes_got.at[tile], vote_ss, vote_rs)
+                to_tile(peer, votes_sent.at[peer], votes_got.at[tile], vote_ss, vote_rs.at[y])
     votes_got[tile] = votes_sent[tile]
 
     short = chans - LANES
@@ -390,16 +396,36 @@
     settle(votes_got.at[rest], vote_ss)
     leave.wait()
 
-    settle(votes_got.at[rest], vote_rs)
-    head = votes_got[:, :CAP, :].reshape(tiles * CAP, LANES)
-    tail = votes_got[:, CAP:, :].astype(F32)
-    tail = jnp.concatenate([tail[:, :, :short], tail[:, :, short:]], 1).reshape(tiles * CAP, short).astype(BF16)
-    vox_out[...] = mm(sums, jnp.concatenate([head, tail], 1)).T
-
-
-def finish(feat, sums, feat_out, sums_out):
-    feat_out[...] = feat[...].astype(F32)
-    sums_out[...] = sums[...]
+    total = None
+    for y in by_distance(ROWS):
+        row = lax.rem(here + ROWS - y, ROWS)
+        settle(votes_got.at[pl.ds(0, deep if y else deep - 1)], vote_rs.at[y])
+        got = votes_got[pl.ds(row * deep, deep)]
+        head = got[:, :CAP, :].reshape(deep * CAP, LANES)
+        tail = got[:, CAP:, :].astype(F32)
+        tail = jnp.concatenate([tail[:, :, :short], tail[:, :, short:]], 1).reshape(deep * CAP, short).astype(BF16)
+        part = mm(sums_of[row], jnp.concatenate([head, tail], 1))
+        total = part if total is None else total + part
+    vox_out[...] = total.T
+
+
+def finish(feat, sums, feat_out, sums_out, feat_near, feat_wide, sums_near, loads, stores):
+    pieces = [pl.ds(i * PIECE, PIECE) for i in range(feat.shape[0] // PIECE)]
+    last = len(pieces)
+    ins = [pltpu.make_async_copy(feat.at[p], feat_near.at[p], loads.at[i]) for i, p in enumerate(pieces)]
+    ins.append(pltpu.make_async_copy(sums, sums_near, loads.at[last]))
+    outs = [pltpu.make_async_copy(feat_wide.at[p], feat_out.at[p], stores.at[i]) for i, p in enumerate(pieces)]
+    outs.append(pltpu.make_async_copy(sums_near, sums_out, stores.at[last]))
+    for copy in ins:
+        copy.start()
+    for i, p in enumerate(pieces):
+        ins[i].wait()
+        feat_wide[p] = feat_near[p].astype(F32)
+        outs[i].start()
+    ins[last].wait()
+    outs[last].start()
+    for copy in outs:
+        copy.wait()
 
 
 def body(
@@ -411,6 +437,7 @@
     groups, tiles = lax.axis_size("grp"), lax.axis_size("tile")
     chunks = slots // groups // WIN
     vmem = pl.BlockSpec(memory_space=pltpu.VMEM)
+    hbm = pl.BlockSpec(memory_space=pltpu.HBM)
     inputs = (
         nodes.T, node_ids.reshape(slots // LANES, LANES), pos_weight,
         gain_one.reshape(1, chans), qkv_one, out_one, gain_two.reshape(1, chans), qkv_two, out_two,
@@ -450,10 +477,11 @@
             pltpu.VMEM((tiles, 8, LANES), F32),
             pltpu.VMEM((tiles, CAP * 3 // 2, LANES), BF16),
             pltpu.VMEM((tiles, CAP * 3 // 2, LANES), BF16),
-            dma, dma, dma, dma, dma, dma((chunks,)), dma, dma((chunks,)), dma, dma,
+            dma, dma, dma, dma, dma, dma((chunks,)), dma, dma((chunks,)), dma, dma((ROWS,)),
             pltpu.SemaphoreType.REGULAR((tiles.bit_length() - 1,)),
             pltpu.VMEM((chans, slots), BF16),
             dma,
+            pltpu.VMEM((ROWS, VOX_DEV, tiles // ROWS * CAP), BF16),
         ],
         compiler_params=pltpu.CompilerParams(collective_id=0, has_side_effects=True),
     )(
@@ -465,8 +493,15 @@
             jax.ShapeDtypeStruct((chans, slots), F32),
             jax.ShapeDtypeStruct((chans, VOX_DEV), F32),
         ),
-        in_specs=[vmem, vmem],
-        out_specs=(vmem, vmem),
+        in_specs=[hbm, hbm],
+        out_specs=(hbm, hbm),
+        scratch_shapes=[
+            pltpu.VMEM((chans, slots), BF16),
+            pltpu.VMEM((chans, slots), F32),
+            pltpu.VMEM((chans, VOX_DEV), F32),
+            dma((chans // PIECE + 1,)),
+            dma((chans // PIECE + 1,)),
+        ],
     )(feat, sums)
     return feat.T, sums.T
 

time: 47.3 us -> 43.9 us (0.928)
  Pallas kernels: 45.8 us -> 42.5 us
    pallas_call x1, Pallas kernels: 43.8 us -> 40.6 us  [body(): pl.pallas_call(functools.partial(kernel, groups=groups, tiles=tiles), out...]
where the time goes in v6:
time: 43.9 us; the launch traced here: 43.8 us
  Pallas kernels  42.5 us (97%)
  between operations  1.29 us (3%)
    pallas_call x1, Pallas kernels, body(): pl.pallas_call(functools.partial(kernel, groups=groups, tiles=tiles), out...  40.6 us
    pallas_call x1, Pallas kernels, body(): pl.pallas_call(finish, out_shape=(jax.ShapeDtypeStruct((chans, slots), F3...  1.93 us

profile of v6, /device:TPU:1, one launch (start us, length us, event | category | flops | bytes accessed | tf_op | source)
XLA Modules:
  0.0 43.8 jit_solution(100058239511795014)
XLA Ops:
  1.3 40.6 %shard_map.167 = (bf16[192,1024]{1,0:T(8,128)(2,1)}, f32[192,256]{1,0:T(8,128)}) custom-call(s32[1]{0:T(128)S(6)} %copy.18.count_ref, bf16[192,1024]{1,0:T(8,128)(2,1)} %bitcast.11, s32[8,128]{1,0:T(8,128)} %bitcast.13, f32[3,192]{1,0:T(4,128)} %refs_2_.1, f32[1,192]{1,0:T(1,128)} %bitcast.17, bf16[192,576]{1,0:T(8,128)(2,1)} %refs_4_.1, ...), custom_call_target="tpu_custom_call" | custom-call | tf_op jit(solution)/shard_map/pallas_call | solution.py:450
  41.8 1.9 %shard_map.168 = (f32[192,1024]{1,0:T(8,128)}, f32[192,256]{1,0:T(8,128)}) custom-call(bf16[192,1024]{1,0:T(8,128)(2,1)} %get-tuple-element.6.feat, f32[192,256]{1,0:T(8,128)} %get-tuple-element.7.sums), custom_call_target="tpu_custom_call" | custom-call | tf_op jit(solution)/shard_map/pallas_call | solution.py:490

commit v7 on v6

--- a/solution.py
+++ b/solution.py
@@ -49,50 +49,48 @@
 def attend(x, biases, gain, w_qkv, w_out):
     chans = x.shape[0]
     dim = chans // HEADS
-    wins = LANES // WIN
     qkv = mm(w_qkv, normed(x, gain))
     query = (qkv[:chans] * (dim**-0.5 * LOG2E)).astype(BF16)
     keys = qkv[chans : 2 * chans].astype(BF16)
     values = qkv[2 * chans :].astype(BF16)
-    lane_win = iota((WIN, LANES), 1) // WIN
-    own = [lane_win == w for w in range(wins)]
-    own_short = [m[:dim] for m in own]
-    zero = jnp.zeros((dim, LANES), BF16)
+    mid = LANES // 2
+    upper = iota((WIN, LANES), 1) >= mid
+    odd = iota((WIN, LANES), 1) // WIN % 2 == 1
+    none = jnp.zeros((WIN, LANES), BF16)
+    short, slim = jnp.zeros((2 * dim, LANES), BF16), none[:dim]
     pairs = [(half, first) for half in range(len(biases)) for first in range(0, HEADS, 2)]
     scores = {}
     for half, first in pairs:
         lanes = slice(LANES * half, LANES * half + LANES)
-        rows = slice(first * dim, first * dim + 2 * dim)
-        two = query[rows, lanes]
-        blocks = jnp.concatenate(
-            [jnp.concatenate([two[:dim], zero], 1), jnp.concatenate([zero, two[dim:]], 1)], 0
-        )
-        full = mm(keys[rows, lanes], blocks, TN)
+        blocks, stacked = [], []
+        for i in range(2):
+            rows = slice((first + i) * dim, (first + i) * dim + dim)
+            mine = query[rows, lanes]
+            split = jnp.concatenate(
+                [jnp.where(upper[:dim], slim, mine), jnp.where(upper[:dim], mine, slim)], 0
+            )
+            blocks.append(jnp.concatenate([short, split] if i else [split, short], 1))
+            stacked += [keys[rows, lanes][:, :mid], keys[rows, lanes][:, mid:]]
+        full = mm(jnp.concatenate(stacked, 0), jnp.concatenate(blocks, 0), TN)
         for i in range(2):
             wide = full[:, LANES * i : LANES * i + LANES]
-            picked = wide[:WIN]
-            for w in range(1, wins):
-                picked = jnp.where(own[w], wide[WIN * w : WIN * w + WIN], picked)
-            scores[half, first + i] = picked + biases[half]
+            scores[half, first + i] = jnp.where(odd, wide[WIN:], wide[:WIN]) + biases[half]
     probs, totals = {}, {}
     for key, score in scores.items():
         weights = jnp.exp2(score - jnp.max(score, 0, keepdims=True))
         totals[key] = 1.0 / jnp.sum(weights, 0, keepdims=True)
-        probs[key] = weights.astype(BF16)
+        weights = weights.astype(BF16)
+        probs[key] = jnp.concatenate([jnp.where(odd, none, weights), jnp.where(odd, weights, none)], 0)
     context = {}
     for half, first in pairs:
-        rows = slice(first * dim, first * dim + 2 * dim)
-        stacked = jnp.concatenate(
-            [values[rows, LANES * half + WIN * w : LANES * half + WIN * w + WIN] for w in range(wins)], 0
-        )
+        lanes = slice(LANES * half, LANES * half + LANES)
+        mine = values[first * dim : first * dim + 2 * dim, lanes]
+        stacked = jnp.concatenate([mine[:, :mid], mine[:, mid:]], 0)
         mixed = mm(stacked, jnp.concatenate([probs[half, first], probs[half, first + 1]], 1))
         for i in range(2):
             wide = mixed[:, LANES * i : LANES * i + LANES]
-            at = [2 * dim * w + dim * i for w in range(wins)]
-            picked = wide[at[0] : at[0] + dim]
-            for w in range(1, wins):
-                picked = jnp.where(own_short[w], wide[at[w] : at[w] + dim], picked)
-            context[half, first + i] = (picked * totals[half, first + i]).astype(BF16)
+            low, high = wide[dim * i : dim * i + dim], wide[dim * (i + 2) : dim * (i + 3)]
+            context[half, first + i] = (jnp.where(upper[:dim], high, low) * totals[half, first + i]).astype(BF16)
     merged = jnp.concatenate(
         [jnp.concatenate([context[half, h] for h in range(HEADS)], 0) for half in range(len(biases))], 1
     )
@@ -224,9 +222,10 @@
     def settle(ref, sem):
         pltpu.make_async_copy(ref, ref, sem).wait()
 
-    def send_one(c):
+    def send_one(step):
+        both = pl.ds(step * UNROLL, UNROLL)
         for d in range(1, groups):
-            to_group(d, sent_one.at[c, grp_peer(d)], got_one.at[c, me], one_ss, one_rs.at[c])
+            to_group(d, sent_one.at[both, grp_peer(d)], got_one.at[both, me], one_ss, one_rs.at[step])
 
     others = pl.ds(0, groups - 1)
     rest = pl.ds(0, tiles - 1)
@@ -263,7 +262,7 @@
 
         for c in here:
             got_one[c, me] = sent_one[c, me]
-            send_one(c)
+        send_one(step)
         return carry
 
     lax.fori_loop(0, chunks // UNROLL, stage_one, 0)
@@ -276,6 +275,46 @@
     up_turned[...] = turned(w_up[...])
     for norm, gain in ((norm_two, gain_two), (norm_three, gain_three)):
         norm[...] = jnp.broadcast_to(gain[...], (LANES, chans)).T
+    told(2)
+    tell(3)
+
+    settle(count_got.at[others], count_rs)
+    counts = jnp.zeros((WIN, LANES), jnp.int32)
+    for g in range(groups):
+        counts = jnp.where(key // run == g, count_got[g][:1, :], counts)
+
+    def stage_two(step, carry):
+        here = [step * UNROLL_TWO + u for u in range(UNROLL_TWO)]
+
+        @pl.when(lax.rem(step * UNROLL_TWO, UNROLL) == 0)
+        def _():
+            both = pl.ds(step * UNROLL_TWO, UNROLL)
+            settle(got_one.at[both, others], one_rs.at[step * UNROLL_TWO // UNROLL])
+
+        for c in here:
+            x = swapped(got_one[c].reshape(rows, chans).astype(F32), groups).T
+            biases = []
+            for half in range(rows // LANES):
+                slot = me * block + c * WIN + (half * (LANES // WIN) + window) * run + key % run
+                kept = jnp.where(slot < counts, 1.0, 0.0)
+                biases.append((kept - 1.0) * 1000000000.0)
+            second = attend(x, biases, norm_two[...], in_two[...], proj_two[...])
+            third = feed(second, norm_three[...], up_turned[...], w_down[...])
+            sent_two[c] = swapped(third.T, groups).astype(BF16).reshape(groups, WIN, chans)
+        for c in here:
+            got_two[me, c] = sent_two[c, me]
+            for d in range(1, groups):
+                to_group(d, sent_two.at[c, grp_peer(d)], got_two.at[me, c], two_ss, two_rs.at[c])
+
+        @pl.when(step == 0)
+        def _():
+            told(3)
+            tell(4)
+
+        return carry
+
+    lax.fori_loop(0, chunks // UNROLL_TWO, stage_two, 0)
+
     votes = owner_ref.shape[1]
     owner = owner_ref[...].astype(F32)
     owner_col = columns(owner)
@@ -295,48 +334,9 @@
     for t in range(tiles):
         vox_sent[t] = jnp.broadcast_to(table[t : t + 1, :], vox_sent.shape[1:])
     vox_got[tile] = vox_sent[tile]
-    told(2)
-    tell(3)
-
-    settle(count_got.at[others], count_rs)
-    counts = jnp.zeros((WIN, LANES), jnp.int32)
-    for g in range(groups):
-        counts = jnp.where(key // run == g, count_got[g][:1, :], counts)
-
-    def stage_two(step, carry):
-        here = [step * UNROLL_TWO + u for u in range(UNROLL_TWO)]
-        for c in here:
-            settle(got_one.at[c, others], one_rs.at[c])
-        for c in here:
-            x = swapped(got_one[c].reshape(rows, chans).astype(F32), groups).T
-            biases = []
-            for half in range(rows // LANES):
-                slot = me * block + c * WIN + (half * (LANES // WIN) + window) * run + key % run
-                kept = jnp.where(slot < counts, 1.0, 0.0)
-                biases.append((kept - 1.0) * 1000000000.0)
-            second = attend(x, biases, norm_two[...], in_two[...], proj_two[...])
-            third = feed(second, norm_three[...], up_turned[...], w_down[...])
-            sent_two[c] = swapped(third.T, groups).astype(BF16).reshape(groups, WIN, chans)
-        for c in here:
-            got_two[me, c] = sent_two[c, me]
-            for d in range(1, groups):
-                to_group(d, sent_two.at[c, grp_peer(d)], got_two.at[me, c], two_ss, two_rs.at[c])
-
-        @pl.when(step == 0)
-        def _():
-            told(3)
-            tell(4)
-
-        @pl.when(step == 1)
-        def _():
-            told(4)
-            for d in range(1, tiles):
-                to_tile(tile_peer(d), vox_sent.at[tile_peer(d)], vox_got.at[tile], vox_ss, vox_rs)
-
-        return carry
-
-    lax.fori_loop(0, chunks // UNROLL_TWO, stage_two, 0)
-
+    told(4)
+    for d in range(1, tiles):
+        to_tile(tile_peer(d), vox_sent.at[tile_peer(d)], vox_got.at[tile], vox_ss, vox_rs)
     slot_col = columns(slot_ref[...])
 
     def pick(c):
@@ -349,18 +349,6 @@
         part = jnp.where(kept, got_two[:, c].reshape(rows, chans).astype(F32), 0.0).astype(BF16)
         return mm(jnp.concatenate(chosen, 1), part)
 
-    settle(vox_got.at[rest], vox_rs)
-    vox = iota((VOX_DEV, LANES), 0).astype(F32)
-    sums = []
-    for a in range(tiles // share):
-        mine = vox_got[share * a]
-        for u in range(1, share):
-            mine = mine + vox_got[share * a + u]
-        sums.append((vox == mine[:1, :]).astype(BF16))
-    deep = tiles // ROWS
-    wide = deep // share
-    for q in range(ROWS):
-        sums_of[q] = jnp.concatenate(sums[q * wide : (q + 1) * wide], 1)
     picked = None
     for c in range(chunks):
         settle(got_two.at[others, c], two_rs.at[c])
@@ -368,6 +356,7 @@
         picked = part if picked is None else picked + part
     picked = picked.astype(BF16)
 
+    deep = tiles // ROWS
     here, along = tile // deep, lax.rem(tile, deep)
     line = iota((deep * CAP, votes), 0)
     for y in by_distance(ROWS):
@@ -389,6 +378,17 @@
     turned_feat[...] = feat.T.astype(BF16)
     leave = pltpu.make_async_copy(turned_feat, feat_out, feat_sem)
     leave.start()
+    settle(vox_got.at[rest], vox_rs)
+    vox = iota((VOX_DEV, LANES), 0).astype(F32)
+    sums = []
+    for a in range(tiles // share):
+        mine = vox_got[share * a]
+        for u in range(1, share):
+            mine = mine + vox_got[share * a + u]
+        sums.append((vox == mine[:1, :]).astype(BF16))
+    wide = deep // share
+    for q in range(ROWS):
+        sums_of[q] = jnp.concatenate(sums[q * wide : (q + 1) * wide], 1)
     settle(count_got.at[others], count_ss)
     settle(got_one.at[:, others], one_ss)
     settle(got_two.at[others, :], two_ss)
@@ -477,7 +477,7 @@
             pltpu.VMEM((tiles, 8, LANES), F32),
             pltpu.VMEM((tiles, CAP * 3 // 2, LANES), BF16),
             pltpu.VMEM((tiles, CAP * 3 // 2, LANES), BF16),
-            dma, dma, dma, dma, dma, dma((chunks,)), dma, dma((chunks,)), dma, dma((ROWS,)),
+            dma, dma, dma, dma, dma, dma((chunks // UNROLL,)), dma, dma((chunks,)), dma, dma((ROWS,)),
             pltpu.SemaphoreType.REGULAR((tiles.bit_length() - 1,)),
             pltpu.VMEM((chans, slots), BF16),
             dma,

time: 43.9 us -> 43.4 us (0.989)
  Pallas kernels: 42.5 us -> 42 us
    pallas_call x1, Pallas kernels: 40.6 us -> 40.1 us  [body(): pl.pallas_call(functools.partial(kernel, groups=groups, tiles=tiles), out...]
where the time goes in v7:
time: 43.4 us; the launch traced here: 43.3 us
  Pallas kernels  42 us (97%)
  between operations  1.29 us (3%)
    pallas_call x1, Pallas kernels, body(): pl.pallas_call(functools.partial(kernel, groups=groups, tiles=tiles), out...  40.1 us
    pallas_call x1, Pallas kernels, body(): pl.pallas_call(finish, out_shape=(jax.ShapeDtypeStruct((chans, slots), F3...  1.93 us

profile of v7, /device:TPU:1, one launch (start us, length us, event | category | flops | bytes accessed | tf_op | source)
XLA Modules:
  0.0 43.3 jit_solution(4934250392734635067)
XLA Ops:
  1.3 40.1 %shard_map.167 = (bf16[192,1024]{1,0:T(8,128)(2,1)}, f32[192,256]{1,0:T(8,128)}) custom-call(s32[1]{0:T(128)S(6)} %copy.18.count_ref, bf16[192,1024]{1,0:T(8,128)(2,1)} %bitcast.11, s32[8,128]{1,0:T(8,128)} %bitcast.13, f32[3,192]{1,0:T(4,128)} %refs_2_.1, f32[1,192]{1,0:T(1,128)} %bitcast.17, bf16[192,576]{1,0:T(8,128)(2,1)} %refs_4_.1, ...), custom_call_target="tpu_custom_call" | custom-call | tf_op jit(solution)/shard_map/pallas_call | solution.py:450
  41.4 1.9 %shard_map.168 = (f32[192,1024]{1,0:T(8,128)}, f32[192,256]{1,0:T(8,128)}) custom-call(bf16[192,1024]{1,0:T(8,128)(2,1)} %get-tuple-element.6.feat, f32[192,256]{1,0:T(8,128)} %get-tuple-element.7.sums), custom_call_target="tpu_custom_call" | custom-call | tf_op jit(solution)/shard_map/pallas_call | solution.py:490

commit v8 on v7

--- a/solution.py
+++ b/solution.py
@@ -177,7 +177,7 @@
     run = WIN // groups
     rows = groups * WIN
     count = count_ref[0]
-    steps = [2**i for i in range(tiles.bit_length() - 1)]
+    steps = sorted((2**i for i in range(tiles.bit_length() - 1)), key=lambda n: (n != tiles // 8, n))
 
     def across(step):
         return tile + step - 2 * step * lax.rem(tile // step, 2)
@@ -275,8 +275,6 @@
     up_turned[...] = turned(w_up[...])
     for norm, gain in ((norm_two, gain_two), (norm_three, gain_three)):
         norm[...] = jnp.broadcast_to(gain[...], (LANES, chans)).T
-    told(2)
-    tell(3)
 
     settle(count_got.at[others], count_rs)
     counts = jnp.zeros((WIN, LANES), jnp.int32)
@@ -307,6 +305,11 @@
                 to_group(d, sent_two.at[c, grp_peer(d)], got_two.at[me, c], two_ss, two_rs.at[c])
 
         @pl.when(step == 0)
+        def _():
+            told(2)
+            tell(3)
+
+        @pl.when(step == 1)
         def _():
             told(3)
             tell(4)
@@ -332,7 +335,7 @@
     share = LANES // CAP
     table = jnp.where(iota((tiles, LANES), 1) // CAP == lax.rem(tile, share), table, 0.0)
     for t in range(tiles):
-        vox_sent[t] = jnp.broadcast_to(table[t : t + 1, :], vox_sent.shape[1:])
+        vox_sent[t] = table[t : t + 1, :]
     vox_got[tile] = vox_sent[tile]
     told(4)
     for d in range(1, tiles):
@@ -385,7 +388,7 @@
         mine = vox_got[share * a]
         for u in range(1, share):
             mine = mine + vox_got[share * a + u]
-        sums.append((vox == mine[:1, :]).astype(BF16))
+        sums.append((vox == mine).astype(BF16))
     wide = deep // share
     for q in range(ROWS):
         sums_of[q] = jnp.concatenate(sums[q * wide : (q + 1) * wide], 1)
@@ -473,8 +476,8 @@
             pltpu.VMEM((groups, chunks, WIN, chans), BF16),
             pltpu.VMEM((8, LANES), jnp.int32),
             pltpu.VMEM((groups, 8, LANES), jnp.int32),
-            pltpu.VMEM((tiles, 8, LANES), F32),
-            pltpu.VMEM((tiles, 8, LANES), F32),
+            pltpu.VMEM((tiles, 1, LANES), F32),
+            pltpu.VMEM((tiles, 1, LANES), F32),
             pltpu.VMEM((tiles, CAP * 3 // 2, LANES), BF16),
             pltpu.VMEM((tiles, CAP * 3 // 2, LANES), BF16),
             dma, dma, dma, dma, dma, dma((chunks // UNROLL,)), dma, dma((chunks,)), dma, dma((ROWS,)),

time: 43.4 us -> 43.4 us (level)
  no operation moved by 1% of the time
where the time goes in v8:
time: 43.4 us; the launch traced here: 43.3 us
  Pallas kernels  42 us (97%)
  between operations  1.29 us (3%)
    pallas_call x1, Pallas kernels, body(): pl.pallas_call(functools.partial(kernel, groups=groups, tiles=tiles), out...  40.1 us
    pallas_call x1, Pallas kernels, body(): pl.pallas_call(finish, out_shape=(jax.ShapeDtypeStruct((chans, slots), F3...  1.93 us

profile of v8, /device:TPU:1, one launch (start us, length us, event | category | flops | bytes accessed | tf_op | source)
XLA Modules:
  0.0 43.3 jit_solution(9074865784708463460)
XLA Ops:
  1.3 40.1 %shard_map.167 = (bf16[192,1024]{1,0:T(8,128)(2,1)}, f32[192,256]{1,0:T(8,128)}) custom-call(s32[1]{0:T(128)S(6)} %copy.18.count_ref, bf16[192,1024]{1,0:T(8,128)(2,1)} %bitcast.11, s32[8,128]{1,0:T(8,128)} %bitcast.13, f32[3,192]{1,0:T(4,128)} %refs_2_.1, f32[1,192]{1,0:T(1,128)} %bitcast.17, bf16[192,576]{1,0:T(8,128)(2,1)} %refs_4_.1, ...), custom_call_target="tpu_custom_call" | custom-call | tf_op jit(solution)/shard_map/pallas_call | solution.py:453
  41.3 1.9 %shard_map.168 = (f32[192,1024]{1,0:T(8,128)}, f32[192,256]{1,0:T(8,128)}) custom-call(bf16[192,1024]{1,0:T(8,128)(2,1)} %get-tuple-element.6.feat, f32[192,256]{1,0:T(8,128)} %get-tuple-element.7.sums), custom_call_target="tpu_custom_call" | custom-call | tf_op jit(solution)/shard_map/pallas_call | solution.py:493
